TPU v7x, 256 devices: a whole 4x4x8 slice. The times are simulated.
256 devices in a mesh: mirror: 2 (over y_hi), slab: 64 (over z, y_lo, x), cols: 2 (over core).
Axes of the slice: x: 4, y: 4 (y_hi: 2, y_lo: 2; y = y_hi * 2 + y_lo), z: 8, core: 2. Of those that a mesh axis runs over, the one named last changes fastest.
Arguments:
- right_side: float32 [2, 1024, 65536], P('mirror', 'slab', 'cols'), parts along dimension 2, may hold values from -6 to 6
- analysis: float32 [2, 1024, 1024], P('mirror'), may hold values from -0.1875 to 0.1875
- synthesis: float32 [2, 1024, 1024], P('mirror'), may hold values from -0.1875 to 0.1875
- negated_eigen: float32 [2, 1024], P('mirror'), may hold values from 0.25 to 4
- wave_square: float32 [65536], P(('cols', 'slab')), parts along dimension 0, may hold values from 0.25 to 4
Outputs:
- solution: float32 [2, 1024, 65536], P('mirror', 'slab', 'cols'), parts along dimension 2
There are 2 independent parts, one for each index of `cols`. A program takes and returns all parts, laid end to end along the dimension named above; an argument that names none is the same for every part. Nothing has to cross between parts.
All inputs are finite; a program needn't handle non-finite values.
Results may differ from a plain program's by a relative error of at most 0.0001.
Values sent between devices are 32-bit elements; how exact they have to be, the bound alone decides.
No kernel may reach another device: no remote copies, remote signals or barrier semaphores. Data moves between devices by JAX's collectives and lax.ppermute only.
A program may use at most 64 MiB of HBM per device.

v0:
```python
import jax
import jax.numpy as jnp
from jax import lax
from jax.sharding import PartitionSpec as P


def from_partner(value, axis, bit):
    mask = 2**bit
    pairs = [(source, source ^ mask) for source in range(lax.axis_size(axis))]
    return lax.ppermute(value, axis, pairs)


def mirror_swap(slab_piece):
    return from_partner(slab_piece, "mirror", 0)


def project(column_field, analysis, synthesis, negated_eigen, wave_square):
    coefficients = jnp.dot(
        analysis, column_field, precision=lax.Precision.HIGHEST, preferred_element_type=jnp.float32
    )
    scaled = coefficients / (negated_eigen[:, None] + wave_square[None, :])
    return -jnp.dot(
        synthesis, scaled, precision=lax.Precision.HIGHEST, preferred_element_type=jnp.float32
    )


def shards(right_side, analysis, synthesis, negated_eigen, wave_square):
    own_half = right_side[0]
    parity = lax.axis_index("mirror")
    parity_sign = (1 - 2 * parity).astype(jnp.float32)
    partner = mirror_swap(own_half)
    lower_half = jnp.where(parity == 0, own_half, partner)
    upper_half = jnp.where(parity == 0, partner, own_half)
    folded = (lower_half + parity_sign * upper_half) * 0.5
    columns = lax.all_to_all(folded, "slab", split_axis=1, concat_axis=0, tiled=True)
    solved = project(columns, analysis[0], synthesis[0], negated_eigen[0], wave_square)
    returned = lax.all_to_all(solved, "slab", split_axis=0, concat_axis=1, tiled=True)
    partner_back = mirror_swap(returned)
    even_part = jnp.where(parity == 0, returned, partner_back)
    odd_part = jnp.where(parity == 0, partner_back, returned)
    result = even_part + parity_sign * odd_part
    return result[None]


def solution(mesh):
    return jax.shard_map(
        shards,
        mesh=mesh,
        in_specs=(
            P("mirror", "slab", "cols"),
            P("mirror", None, None),
            P("mirror", None, None),
            P("mirror", None),
            P(("cols", "slab")),
        ),
        out_specs=P("mirror", "slab", "cols"),
        check_vma=False,
    )
```

profile of v0, /device:TPU:36, one launch (start us, length us, event | category | flops | bytes accessed | tf_op | source)
XLA Modules:
  0.0 242.4 jit_solution(17822131640532167315)
XLA Ops:
  0.0 3.2 %collective-permute-start = (f32[16,32768]{1,0:T(8,128)}, f32[16,32768]{1,0:T(8,128)S(1)}, u32[]{:S(2)}, u32[]{:S(2)}) collective-permute-start(f32[16,32768]{1,0:T(8,128)} %bitcast.39), channel_id=1, source_target_pairs={{0,128},{128,0},{1,129},{129,1},{2,130},{130,2},{3,131},{131,3},{4... | collective-permute-start | bytes 6291464 | tf_op jit(solution)/shard_map/ppermute | solution.py:10
  3.2 45.9 %collective-permute-done = f32[16,32768]{1,0:T(8,128)S(1)} collective-permute-done((f32[16,32768]{1,0:T(8,128)}, f32[16,32768]{1,0:T(8,128)S(1)}, u32[]{:S(2)}, u32[]{:S(2)}) %collective-permute-start) | collective-permute-done | bytes 2097184 | tf_op jit(solution)/shard_map/ppermute | solution.py:10
  49.1 1.9 add_multiply_fusion
  51.0 0.2 copy.17
  51.2 0.0 copy-start
  51.3 61.3 %all_to_all.38 = f32[16,64,512]{2,0,1:T(8,128)S(1)} all-to-all(f32[16,64,512]{2,0,1:T(8,128)S(1)} %bitcast.36), channel_id=1, replica_groups=mesh['mirror'=2,'slab'=64,'cols'=2] {'slab'}, dimensions={1} | all-to-all | bytes 4194304 | tf_op jit(solution)/shard_map/all_to_all | solution.py:35
  112.6 0.0 copy-done
  112.6 0.0 copy-start.1
  112.6 0.0 copy-start.2
  112.6 0.0 copy-start.3
  112.6 13.6 %fusion.2 = f32[512,1024]{1,0:T(8,128)S(1)} fusion(f32[1024,512]{1,0:T(8,128)S(1)} %bitcast.32, f32[1,1024,1024]{2,1,0:T(8,128)S(1)} %copy-done), kind=kOutput, calls=%fused_computation.2 | convolution fusion | flops 6442450944 | bytes 8388608 | tf_op jit(solution)/shard_map/dot_general | solution.py:18
  126.2 0.0 copy-done.1
  126.2 0.0 copy-done.2
  126.2 0.0 copy-done.3
  126.2 8.4 %negate_bitcast_fusion = f32[1024,512]{0,1:T(8,128)} fusion(f32[1,1024,1024]{2,1,0:T(8,128)S(1)} %copy-done.1, f32[512,1024]{1,0:T(8,128)S(1)} %fusion.2, f32[512]{0:T(512)S(1)} %copy-done.3, f32[1024]{0:T(1024)S(1)} %bitcast.40), kind=kOutput, calls=%fused_computation.7 | convolution fusion | flops 6444023808 | bytes 8394752 | tf_op jit(solution)/shard_map/dot_general | solution.py:22
  134.6 1.9 copy.12
  136.6 56.0 %all_to_all.39 = f32[64,16,512]{2,1,0:T(8,128)S(1)} all-to-all(f32[64,16,512]{2,1,0:T(8,128)S(1)} %bitcast.37), channel_id=1, replica_groups=mesh['mirror'=2,'slab'=64,'cols'=2] {'slab'}, dimensions={0} | all-to-all | bytes 4194304 | tf_op jit(solution)/shard_map/all_to_all | solution.py:37
  192.5 0.2 copy.15
  192.7 3.0 %collective-permute-start.1 = (f32[16,32768]{1,0:T(8,128)S(1)}, f32[16,32768]{1,0:T(8,128)S(1)}, u32[]{:S(2)}, u32[]{:S(2)}) collective-permute-start(f32[16,32768]{1,0:T(8,128)S(1)} %bitcast.33), channel_id=1, source_target_pairs={{0,128},{128,0},{1,129},{129,1},{2,130},{130,2},{3,131},{131,3},{4... | collective-permute-start | bytes 6291464 | tf_op jit(solution)/shard_map/ppermute | solution.py:10
  195.7 45.2 %collective-permute-done.1 = f32[16,32768]{1,0:T(8,128)S(1)} collective-permute-done((f32[16,32768]{1,0:T(8,128)S(1)}, f32[16,32768]{1,0:T(8,128)S(1)}, u32[]{:S(2)}, u32[]{:S(2)}) %collective-permute-start.1) | collective-permute-done | bytes 2097184 | tf_op jit(solution)/shard_map/ppermute | solution.py:10
  240.8 1.6 add_bitcast_fusion
Async XLA Ops:
  0.0 49.1 %collective-permute-start = (f32[16,32768]{1,0:T(8,128)}, f32[16,32768]{1,0:T(8,128)S(1)}, u32[]{:S(2)}, u32[]{:S(2)}) collective-permute-start(f32[16,32768]{1,0:T(8,128)} %bitcast.39), channel_id=1, source_target_pairs={{0,128},{128,0},{1,129},{129,1},{2,130},{130,2},{3,131},{131,3},{4... | collective-permute-start | bytes 6291464 | tf_op jit(solution)/shard_map/ppermute | solution.py:10
  51.2 61.3 %copy-start = (f32[1,1024,1024]{2,1,0:T(8,128)S(1)}, f32[1,1024,1024]{2,1,0:T(8,128)}, u32[]{:S(2)}) copy-start(f32[1,1024,1024]{2,1,0:T(8,128)} %param.6) | copy-start | bytes 12582916
  112.6 13.7 %copy-start.1 = (f32[1,1024,1024]{2,1,0:T(8,128)S(1)}, f32[1,1024,1024]{2,1,0:T(8,128)}, u32[]{:S(2)}) copy-start(f32[1,1024,1024]{2,1,0:T(8,128)} %param.7) | copy-start | bytes 12582916
  112.6 13.7 %copy-start.2 = (f32[1,1024]{1,0:T(1,128)S(1)}, f32[1,1024]{1,0:T(1,128)}, u32[]{:S(2)}) copy-start(f32[1,1024]{1,0:T(1,128)} %param.8) | copy-start | bytes 12292
  112.6 13.7 %copy-start.3 = (f32[512]{0:T(512)S(1)}, f32[512]{0:T(512)}, u32[]{:S(2)}) copy-start(f32[512]{0:T(512)} %param.9) | copy-start | bytes 6148
  192.7 48.1 %collective-permute-start.1 = (f32[16,32768]{1,0:T(8,128)S(1)}, f32[16,32768]{1,0:T(8,128)S(1)}, u32[]{:S(2)}, u32[]{:S(2)}) collective-permute-start(f32[16,32768]{1,0:T(8,128)S(1)} %bitcast.33), channel_id=1, source_target_pairs={{0,128},{128,0},{1,129},{129,1},{2,130},{130,2},{3,131},{131,3},{4... | collective-permute-start | bytes 6291464 | tf_op jit(solution)/shard_map/ppermute | solution.py:10
where the time goes:
time: 243 us; the launch traced here: 242 us
  blocking collectives  117 us (48%)
  waiting for transfers between devices  91 us (37%)
  matrix products  22 us (9%)
  starting transfers between devices  6.18 us (3%)
  other arithmetic  3.53 us (1%)
    ppermute x2, waiting for transfers between devices, from_partner(): return lax.ppermute(value, axis, pairs)  91 us
    all_to_all x1, blocking collectives, shards(): lax.all_to_all(folded, 'slab', split_axis=1, concat_axis=0, tiled=True)  61.3 us
    all_to_all x1, blocking collectives, shards(): lax.all_to_all(solved, 'slab', split_axis=0, concat_axis=1, tiled=True)  56 us
    dot_general x1, matrix products, project(): jnp.dot(analysis, column_field, precision=lax.Precision.HIGHEST, preferre...  13.6 us
    dot_general x1, matrix products, project(): jnp.dot(synthesis, scaled, precision=lax.Precision.HIGHEST, preferred_ele...  8.39 us
    ppermute x2, starting transfers between devices, from_partner(): return lax.ppermute(value, axis, pairs)  6.18 us
  transfers between devices with their start and end apart: 2, of which 2 were waited for; matrix products, arithmetic and copies ran while one was open for 0% of the time, Pallas kernels for 0%

commit v1 on v0

v1 whole, which is shorter than its diff:
```python
import jax
import jax.numpy as jnp
from jax import lax
from jax.experimental import pallas as pl
from jax.experimental.pallas import tpu as pltpu
from jax.sharding import PartitionSpec as P


Z, YL, X = 8, 2, 4
ZX = Z * X
ROWS, COLS = 16, 256
POINTS = Z * YL * X * ROWS
WIDE = Z * YL * X * 2 * COLS
MIB = 1024 * 1024
F32, BF16 = jnp.float32, jnp.bfloat16
VMEM = pl.BlockSpec(memory_space=pltpu.VMEM)
ANY = pl.BlockSpec(memory_space=pltpu.HBM)
PART = jax.ShapeDtypeStruct((ZX, ROWS, COLS), F32)
WHOLE = jax.ShapeDtypeStruct((ZX, YL, ROWS, COLS), F32)
CHUNKS = 4
STEP = POINTS // CHUNKS
GRANT = 58


def call(kernel, inputs, outs, scratch=(), flops=0, grant=8, in_any=0, out_any=False):
    size = sum(v.size * 4 for v in (*inputs, *outs))
    return pl.pallas_call(
        kernel,
        out_shape=tuple(outs),
        in_specs=[ANY] * in_any + [VMEM] * (len(inputs) - in_any),
        out_specs=tuple([ANY if out_any else VMEM] * len(outs)),
        scratch_shapes=list(scratch),
        compiler_params=pltpu.CompilerParams(vmem_limit_bytes=grant * MIB),
        cost_estimate=pl.CostEstimate(flops=flops, bytes_accessed=size, transcendentals=0),
    )(*inputs)


def y_low():
    return (lax.axis_index("slab") >> 2) & 1


def signs():
    high, low = lax.axis_index("mirror"), y_low()
    own = 1 - 2 * high
    above = 1 - 2 * high * (1 - low)
    below = 1 - 2 * high * low
    return own.astype(F32), above.astype(F32), below.astype(F32)


def block_of(low, at):
    return (at // X) * YL * X + low * X + at % X


def open_kernel(x_hbm, b_ref, own_ref, other_ref, x_ref, sems):
    low = y_low()
    width = WIDE // CHUNKS
    copies = []
    for c in range(CHUNKS):
        cols = pl.ds(c * width, width)
        copies.append(pltpu.make_async_copy(x_hbm.at[:, :, cols], x_ref.at[:, :, cols], sems.at[c]))
        copies[-1].start()
    for at in range(ZX):
        if at % (ZX // CHUNKS) == 0:
            copies[at // (ZX // CHUNKS)].wait()
        for yl in range(YL):
            col = block_of(yl, at) * 2 * COLS
            b_ref[at, yl] = x_ref[0, :, col + COLS : col + 2 * COLS]
        base = (at // X) * YL * X + at % X
        for ref, half in ((own_ref, low), (other_ref, 1 - low)):
            col = pl.multiple_of((base + half * X) * 2 * COLS, COLS)
            ref[at] = x_ref[0, :, pl.ds(col, COLS)]


def pick_kernel(in_ref, own_ref, other_ref):
    low = y_low()
    for at in range(ZX):
        own_ref[at] = in_ref[at, low]
        other_ref[at] = in_ref[at, 1 - low]


def joined(own_ref, across_ref, above_ref, below_ref, at):
    own_sign, above_sign, below_sign = signs()
    near = across_ref[at] + own_sign * own_ref[at]
    far = above_sign * above_ref[at] + below_sign * below_ref[at]
    return near, far


def fold_kernel(own_ref, across_ref, above_ref, below_ref, out_ref):
    low = y_low()
    for at in range(ZX):
        near, far = joined(own_ref, across_ref, above_ref, below_ref, at)
        out_ref[at, low] = near
        out_ref[at, 1 - low] = far


def split(value):
    high = value.astype(BF16)
    return high, (value - high.astype(F32)).astype(BF16)


def split_kernel(a_ref, s_ref, *outs):
    @pl.loop(0, POINTS // 64)
    def _(step):
        rows = pl.ds(pl.multiple_of(step * 64, 64), 64)
        outs[0][rows], outs[1][rows] = split(a_ref[0, rows])
        outs[2][rows], outs[3][rows] = split(s_ref[0, rows])


def product(high, low, high_ref, low_ref):
    def dot(a, b):
        return jnp.dot(a, b, preferred_element_type=F32)

    return dot(high, high_ref[...]) + (dot(high, low_ref[...]) + dot(low, high_ref[...]))


def row_of(low, at):
    return block_of(low, at) * ROWS


def chunk(sources, held, sems, i, c):
    rows = pl.ds(pl.multiple_of(c * STEP, STEP), STEP)
    return pltpu.make_async_copy(sources[i].at[rows], held[i].at[rows], sems.at[i, c])


def fetch(sources, held, sems):
    for m in (0, 2):
        for c in range(CHUNKS):
            for i in (m, m + 1):
                chunk(sources, held, sems, i, c).start()


def solve(sources, held, sems, neg_ref, wave, fh, fl, ch, cl, done):
    @pl.loop(0, CHUNKS)
    def _(c):
        chunk(sources, held, sems, 0, c).wait()
        chunk(sources, held, sems, 1, c).wait()
        rows = pl.ds(pl.multiple_of(c * STEP, STEP), STEP)
        coefficients = product(held[0][rows], held[1][rows], fh, fl)
        ch[rows], cl[rows] = split(coefficients / (neg_ref[rows] + wave))

    @pl.loop(0, CHUNKS)
    def _(c):
        chunk(sources, held, sems, 2, c).wait()
        chunk(sources, held, sems, 3, c).wait()
        rows = pl.ds(pl.multiple_of(c * STEP, STEP), STEP)
        done[rows] = -product(held[2][rows], held[3][rows], ch, cl)


def solve_a_kernel(*refs):
    sources, (neg_ref, wave_ref, in_ref, out_ref) = refs[:4], refs[4:8]
    held, sems, work = refs[8:12], refs[12], refs[13:]
    fetch(sources, held, sems)
    fh, fl, _, _, done = work
    for at in range(ZX):
        for yl in range(YL):
            rows = pl.ds(row_of(yl, at), ROWS)
            fh[rows], fl[rows] = split(in_ref[at, yl] * 0.5)
    solve(sources, held, sems, neg_ref, wave_ref[:, :COLS], *work)
    for at in range(ZX):
        for yl in range(YL):
            out_ref[at, yl] = done[pl.ds(row_of(yl, at), ROWS)]


def solve_b_kernel(*refs):
    sources, (neg_ref, wave_ref, own_in, across, above, below) = refs[:4], refs[4:10]
    own_out, other_out = refs[10:12]
    held, sems, work = refs[12:16], refs[16], refs[17:]
    fetch(sources, held, sems)
    fh, fl, _, _, done = work
    low = y_low()

    def rows_of(half, at):
        base = ((at // X) * YL * X + at % X) * ROWS
        return pl.ds(pl.multiple_of(base + half * (X * ROWS), ROWS), ROWS)

    for at in range(ZX):
        near, far = joined(own_in, across, above, below, at)
        for half, value in ((low, near), (1 - low, far)):
            rows = rows_of(half, at)
            fh[rows], fl[rows] = split(value * 0.5)
    solve(sources, held, sems, neg_ref, wave_ref[:, COLS:], *work)
    for at in range(ZX):
        own_out[at] = done[rows_of(low, at)]
        other_out[at] = done[rows_of(1 - low, at)]


def close_kernel(b_ref, own_ref, across_ref, above_ref, below_ref, out_ref, held, sems):
    low = y_low()
    copies = []
    for z in range(Z):
        for at in range(z * X, z * X + X):
            near, far = joined(own_ref, across_ref, above_ref, below_ref, at)
            base = (at // X) * YL * X + at % X
            for half, value in ((low, near), (1 - low, far)):
                col = pl.multiple_of((base + half * X) * 2 * COLS, COLS)
                held[:, pl.ds(col, COLS)] = value
            for yl in range(YL):
                col = block_of(yl, at) * 2 * COLS + COLS
                held[:, col : col + COLS] = b_ref[at, yl]
        cols = pl.ds(z * YL * X * 2 * COLS, YL * X * 2 * COLS)
        copies.append(pltpu.make_async_copy(held.at[:, cols], out_ref.at[0, :, cols], sems.at[z]))
        copies[-1].start()
    for copy in copies:
        copy.wait()


def zx_exchange(blocks):
    groups = [[(z * YL + yl) * X + x for z in range(Z) for x in range(X)] for yl in range(YL)]
    return lax.all_to_all(
        blocks, "slab", split_axis=0, concat_axis=0, axis_index_groups=groups, tiled=True
    )


def y_move(block, hop):
    def device(y, z, x):
        return (y // YL) * Z * YL * X + (z * YL + y % YL) * X + x

    every = [(y, z, x) for y in range(2 * YL) for z in range(Z) for x in range(X)]
    pairs = [(device(y, z, x), device((y + hop) % 4, z, x)) for y, z, x in every]
    return lax.ppermute(block, ("mirror", "slab"), pairs)


def y_exchange(own, other):
    across = y_move(own, 2)
    above = y_move(other, 3)
    below = y_move(other, 1)
    return own, across, above, below


def body(right_side, analysis, synthesis, negated_eigen, wave_square):
    work = [
        *[pltpu.VMEM((POINTS, POINTS), BF16)] * 4,
        pltpu.SemaphoreType.DMA((4, CHUNKS)),
        *[pltpu.VMEM((POINTS, COLS), BF16)] * 4,
        pltpu.VMEM((POINTS, COLS), F32),
    ]
    flops = 12 * POINTS * POINTS * COLS
    half = jax.ShapeDtypeStruct((POINTS, POINTS), BF16)
    matrices = call(split_kernel, [analysis, synthesis], [half] * 4)
    levels = (*matrices, negated_eigen.reshape(POINTS, 1), wave_square.reshape(1, 2 * COLS))
    held = [pltpu.VMEM((ROWS, WIDE), F32), pltpu.SemaphoreType.DMA((Z,))]

    stage = [pltpu.VMEM((1, ROWS, WIDE), F32), pltpu.SemaphoreType.DMA((CHUNKS,))]

    b, *a = call(open_kernel, [right_side], [WHOLE, PART, PART], stage, 0, GRANT, 1)
    b = zx_exchange(b)
    a = y_exchange(*a)
    (a,) = call(fold_kernel, a, [WHOLE])
    b = call(pick_kernel, [b], [PART, PART])
    a = zx_exchange(a)
    b = y_exchange(*b)
    b = call(solve_b_kernel, [*levels, *b], [PART, PART], work, flops, GRANT, 4)
    (a,) = call(solve_a_kernel, [*levels, a], [WHOLE], work, flops, GRANT, 4)
    a = zx_exchange(a)
    b = y_exchange(*b)
    (b,) = call(fold_kernel, b, [WHOLE])
    a = call(pick_kernel, [a], [PART, PART])
    b = zx_exchange(b)
    a = y_exchange(*a)
    out = jax.ShapeDtypeStruct((1, ROWS, WIDE), F32)
    return call(close_kernel, [b, *a], [out], held, out_any=True)[0]


def solution(mesh):
    return jax.shard_map(
        body,
        mesh=mesh,
        in_specs=(
            P("mirror", "slab", "cols"),
            P("mirror", None, None),
            P("mirror", None, None),
            P("mirror", None),
            P(("cols", "slab")),
        ),
        out_specs=P("mirror", "slab", "cols"),
        check_vma=False,
    )
```

time: 243 us -> 212 us (0.87)
  blocking collectives: 117 us -> 38 us
  starting transfers between devices: 6.18 us -> 44.4 us
  Pallas kernels: 0 us -> 24.1 us
  matrix products: 22 us -> 0 us
  local copies, waits for them, and re-layouts: 2.33 us -> 13.8 us
  other arithmetic: 3.53 us -> 0 us
    all_to_all x2 -> x1, blocking collectives: 117 us -> 38 us  [zx_exchange(): lax.all_to_all(blocks, 'slab', split_axis=0, concat_axis=0, axis_index_gr...]
    pallas_call x0 -> x9, Pallas kernels: none -> 24.1 us  [call(): pl.pallas_call(kernel, out_shape=tuple(outs), in_specs=[ANY] * in_any + [...]
    all_to_all x0 -> x3, starting transfers between devices: none -> 22.7 us  [zx_exchange(): lax.all_to_all(blocks, 'slab', split_axis=0, concat_axis=0, axis_index_gr...]
    dot_general x2 -> x0, matrix products: 22 us -> none  [the longest x1 13.6 us: project(): jnp.dot(analysis, column_field, precision=lax.Precision.HIGHEST, preferre...]
    ppermute x2 -> x12, starting transfers between devices: 6.18 us -> 21.7 us  [y_move(): return lax.ppermute(block, ('mirror', 'slab'), pairs)]
    unnamed x8 -> x26, local copies, waits for them, and re-layouts: 0.02 us -> 12.7 us
    ppermute x2 -> x12, waiting for transfers between devices: 91 us -> 83.4 us  [y_move(): return lax.ppermute(block, ('mirror', 'slab'), pairs)]
    all_to_all x0 -> x3, waiting for transfers between devices: none -> 6.56 us  [zx_exchange(): lax.all_to_all(blocks, 'slab', split_axis=0, concat_axis=0, axis_index_gr...]
  transfers between devices with their start and end apart: 2 -> 15, of which waited for: 2 -> 12; matrix products, arithmetic and copies ran while one was open for 0% -> 0% of each run, Pallas kernels for 0% -> 9%
where the time goes in v1:
time: 212 us; the launch traced here: 210 us
  waiting for transfers between devices  90 us (42%)
  starting transfers between devices  44.4 us (21%)
  blocking collectives  38 us (18%)
  Pallas kernels  24.1 us (11%)
  local copies, waits for them, and re-layouts  13.8 us (7%)
    ppermute x12, waiting for transfers between devices, y_move(): return lax.ppermute(block, ('mirror', 'slab'), pairs)  83.4 us
    all_to_all x1, blocking collectives, zx_exchange(): lax.all_to_all(blocks, 'slab', split_axis=0, concat_axis=0, axis_index_gr...  38 us
    pallas_call x9, Pallas kernels, call(): pl.pallas_call(kernel, out_shape=tuple(outs), in_specs=[ANY] * in_any + [...  24.1 us
    all_to_all x3, starting transfers between devices, zx_exchange(): lax.all_to_all(blocks, 'slab', split_axis=0, concat_axis=0, axis_index_gr...  22.7 us
    ppermute x12, starting transfers between devices, y_move(): return lax.ppermute(block, ('mirror', 'slab'), pairs)  21.7 us
    unnamed x26, local copies, waits for them, and re-layouts  12.7 us
    all_to_all x3, waiting for transfers between devices, zx_exchange(): lax.all_to_all(blocks, 'slab', split_axis=0, concat_axis=0, axis_index_gr...  6.56 us
  transfers between devices with their start and end apart: 15, of which 12 were waited for; matrix products, arithmetic and copies ran while one was open for 0% of the time, Pallas kernels for 9%

profile of v1, /device:TPU:36, one launch (start us, length us, event | category | flops | bytes accessed | tf_op | source)
XLA Modules:
  0.0 210.4 jit_solution(7852601733131531269)
XLA Ops:
  0.0 2.9 %shard_map.56 = (f32[32,2,16,256]{3,2,1,0:T(8,128)}, f32[32,16,256]{2,1,0:T(8,128)}, f32[32,16,256]{2,1,0:T(8,128)}) custom-call(f32[1,16,32768]{2,1,0:T(8,128)} %x_hbm.1), custom_call_target="tpu_custom_call" | custom-call | bytes 4194304 | tf_op jit(solution)/shard_map/pallas_call | solution.py:27
  2.9 3.3 %collective-permute-start.6 = (f32[32,16,256]{2,1,0:T(8,128)}, f32[32,16,256]{2,1,0:T(8,128)S(1)}, u32[]{:S(2)}, u32[]{:S(2)}) collective-permute-start(f32[32,16,256]{2,1,0:T(8,128)} %get-tuple-element.27.own_ref), channel_id=1, source_target_pairs={{0,128},{2,130},{4,132},{6,134},{16,144},{18,146},{20,148},{22,150... | collective-permute-start | bytes 1572872 | tf_op jit(solution)/shard_map/ppermute | solution.py:220
  6.2 0.7 collective-permute-start.8
  6.8 2.6 %collective-permute-start.7 = (f32[32,16,256]{2,1,0:T(8,128)}, f32[32,16,256]{2,1,0:T(8,128)S(1)}, u32[]{:S(2)}, u32[]{:S(2)}) collective-permute-start(f32[32,16,256]{2,1,0:T(8,128)} %get-tuple-element.28), channel_id=1, source_target_pairs={{0,136},{2,138},{4,140},{6,142},{16,152},{18,154},{20,156},{22,158... | collective-permute-start | bytes 1572872 | tf_op jit(solution)/shard_map/ppermute | solution.py:220
  9.4 10.1 %collective-permute-done.6.across_ref = f32[32,16,256]{2,1,0:T(8,128)S(1)} collective-permute-done((f32[32,16,256]{2,1,0:T(8,128)}, f32[32,16,256]{2,1,0:T(8,128)S(1)}, u32[]{:S(2)}, u32[]{:S(2)}) %collective-permute-start.6) | collective-permute-done | bytes 524320 | tf_op jit(solution)/shard_map/ppermute | solution.py:220
  19.5 10.1 %collective-permute-done.8.below_ref = f32[32,16,256]{2,1,0:T(8,128)S(1)} collective-permute-done((f32[32,16,256]{2,1,0:T(8,128)}, f32[32,16,256]{2,1,0:T(8,128)S(1)}, u32[]{:S(2)}, u32[]{:S(2)}) %collective-permute-start.8) | collective-permute-done | bytes 524320 | tf_op jit(solution)/shard_map/ppermute | solution.py:220
  29.6 0.4 collective-permute-done.7.above_ref
  30.0 0.0 copy-start.3
  30.0 1.0 copy-done.3
  31.0 0.1 shard_map.60
  31.1 0.0 copy-start.9
  31.1 38.0 %all_to_all.20.refs_6_ = f32[32,2,16,256]{3,2,1,0:T(8,128)} all-to-all(f32[32,2,16,256]{3,2,1,0:T(8,128)S(1)} %shard_map.60), channel_id=1, replica_groups={{0,2,4,6,16,18,20,22,32,34,36,38,48,50,52,54,64,66,68,70,80,82,84,86,96..., dimensions={0} | all-to-all | bytes 2097152 | tf_op jit(solution)/shard_map/all_to_all | solution.py:209
  69.2 6.4 %all-to-all-start = ((f32[32,2,16,256]{3,2,1,0:T(8,128)}), f32[32,2,16,256]{3,2,1,0:T(8,128)S(1)}, u32[]{:S(2)}, u32[]{:S(2)}) async-start(f32[32,2,16,256]{3,2,1,0:T(8,128)} %get-tuple-element.22), calls=%async_computation | async-start | bytes 2097152 | tf_op jit(solution)/shard_map/all_to_all | solution.py:209
  75.6 0.0 copy-done.9
  75.6 1.0 copy.6.refs_4_
  76.6 0.0 copy-start
  76.6 2.2 %copy-done = f32[1,1024,1024]{2,1,0:T(8,128)S(1)} copy-done((f32[1,1024,1024]{2,1,0:T(8,128)S(1)}, f32[1,1024,1024]{2,1,0:T(8,128)}, u32[]{:S(2)}) %copy-start) | copy-done | bytes 4194328
  78.8 0.0 copy-start.1
  78.8 2.2 %copy-done.1 = f32[1,1024,1024]{2,1,0:T(8,128)S(1)} copy-done((f32[1,1024,1024]{2,1,0:T(8,128)S(1)}, f32[1,1024,1024]{2,1,0:T(8,128)}, u32[]{:S(2)}) %copy-start.1) | copy-done | bytes 4194328
  81.0 1.3 shard_map.55
  82.4 0.0 copy-start.4
  82.4 1.3 copy-done.4
  83.7 0.0 copy-start.5
  83.7 1.3 copy-done.5
  85.0 0.0 copy-start.6
  85.0 1.3 copy-done.6
  86.4 0.0 copy-start.7
  86.4 1.4 copy-done.7
  87.7 8.4 %shard_map.61 = f32[32,2,16,256]{3,2,1,0:T(8,128)} custom-call(bf16[1024,1024]{1,0:T(8,128)(2,1)} %copy-done.4, bf16[1024,1024]{1,0:T(8,128)(2,1)} %copy-done.5, bf16[1024,1024]{1,0:T(8,128)(2,1)} %copy-done.6, bf16[1024,1024]{1,0:T(8,128)(2,1)} %copy-done.7, f32[1024,1]{1,0:T(8,128)} %copy.6.refs_4_, f32[1,512]{1,0:T(1,128)} %bitcast.3, ...), custom_call_target="tpu_custom_call" | custom-call | flops 3221225472 | bytes 18880512 | tf_op jit(solution)/shard_map/pallas_call | solution.py:27
  96.1 5.4 %all-to-all-done.in_ref = f32[32,2,16,256]{3,2,1,0:T(8,128)S(1)} async-done(((f32[32,2,16,256]{3,2,1,0:T(8,128)}), f32[32,2,16,256]{3,2,1,0:T(8,128)S(1)}, u32[]{:S(2)}, u32[]{:S(2)}) %all-to-all-start) | async-done | bytes 1048608 | tf_op jit(solution)/shard_map/all_to_all | solution.py:209
  101.5 6.4 %all-to-all-start.3 = ((f32[32,2,16,256]{3,2,1,0:T(8,128)}), f32[32,2,16,256]{3,2,1,0:T(8,128)S(1)}, u32[]{:S(2)}, u32[]{:S(2)}) async-start(f32[32,2,16,256]{3,2,1,0:T(8,128)} %shard_map.61), calls=%async_computation.3 | async-start | bytes 2097152 | tf_op jit(solution)/shard_map/all_to_all | solution.py:209
  108.0 0.1 shard_map.57
  108.1 0.0 copy-start.8
  108.1 1.7 collective-permute-start
  109.8 2.4 %collective-permute-start.2 = (f32[32,16,256]{2,1,0:T(8,128)S(1)}, f32[32,16,256]{2,1,0:T(8,128)S(1)}, u32[]{:S(2)}, u32[]{:S(2)}) collective-permute-start(f32[32,16,256]{2,1,0:T(8,128)S(1)} %get-tuple-element.24), channel_id=1, source_target_pairs={{0,8},{2,10},{4,12},{6,14},{16,24},{18,26},{20,28},{22,30},{32,40}... | collective-permute-start | bytes 1572872 | tf_op jit(solution)/shard_map/ppermute | solution.py:220
  112.2 0.8 collective-permute-start.1
  113.0 11.4 %collective-permute-done.refs_7_ = f32[32,16,256]{2,1,0:T(8,128)S(1)} collective-permute-done((f32[32,16,256]{2,1,0:T(8,128)S(1)}, f32[32,16,256]{2,1,0:T(8,128)S(1)}, u32[]{:S(2)}, u32[]{:S(2)}) %collective-permute-start) | collective-permute-done | bytes 524320 | tf_op jit(solution)/shard_map/ppermute | solution.py:220
  124.5 0.0 copy-start.10
  124.5 8.0 %collective-permute-done.2.refs_9_ = f32[32,16,256]{2,1,0:T(8,128)S(1)} collective-permute-done((f32[32,16,256]{2,1,0:T(8,128)S(1)}, f32[32,16,256]{2,1,0:T(8,128)S(1)}, u32[]{:S(2)}, u32[]{:S(2)}) %collective-permute-start.2) | collective-permute-done | bytes 524320 | tf_op jit(solution)/shard_map/ppermute | solution.py:220
  132.4 0.7 collective-permute-done.1.refs_8_
  133.1 0.0 copy-done.8
  133.1 0.0 copy-done.10
  133.1 0.1 copy-done.11
  133.2 0.8 copy-done.12
  134.1 8.7 %shard_map.58 = (f32[32,16,256]{2,1,0:T(8,128)}, f32[32,16,256]{2,1,0:T(8,128)}) custom-call(bf16[1024,1024]{1,0:T(8,128)(2,1)} %copy-done.4, bf16[1024,1024]{1,0:T(8,128)(2,1)} %copy-done.5, bf16[1024,1024]{1,0:T(8,128)(2,1)} %copy-done.6, bf16[1024,1024]{1,0:T(8,128)(2,1)} %copy-done.7, f32[1024,1]{1,0:T(8,128)} %copy.6.refs_4_, f32[1,512]{1,0:T(1,128)} %bitcast.4, ...), custom_call_target="tpu_custom_call" | custom-call | flops 3221225472 | bytes 19929088 | tf_op jit(solution)/shard_map/pallas_call | solution.py:27
  142.8 1.9 collective-permute-start.3
  144.7 1.6 collective-permute-start.5
  146.3 1.6 collective-permute-start.4
  147.9 11.5 %collective-permute-done.3.across_ref = f32[32,16,256]{2,1,0:T(8,128)S(1)} collective-permute-done((f32[32,16,256]{2,1,0:T(8,128)}, f32[32,16,256]{2,1,0:T(8,128)S(1)}, u32[]{:S(2)}, u32[]{:S(2)}) %collective-permute-start.3) | collective-permute-done | bytes 524320 | tf_op jit(solution)/shard_map/ppermute | solution.py:220
  159.4 10.2 %collective-permute-done.5.below_ref = f32[32,16,256]{2,1,0:T(8,128)S(1)} collective-permute-done((f32[32,16,256]{2,1,0:T(8,128)}, f32[32,16,256]{2,1,0:T(8,128)S(1)}, u32[]{:S(2)}, u32[]{:S(2)}) %collective-permute-start.5) | collective-permute-done | bytes 524320 | tf_op jit(solution)/shard_map/ppermute | solution.py:220
  169.7 0.0 collective-permute-done.4.above_ref
  169.7 1.0 copy-done.2
  170.7 1.1 shard_map.59
  171.8 0.0 all-to-all-done.3.in_ref
  171.8 9.8 %all-to-all-start.1 = ((f32[32,2,16,256]{3,2,1,0:T(8,128)}), f32[32,2,16,256]{3,2,1,0:T(8,128)S(1)}, u32[]{:S(2)}, u32[]{:S(2)}) async-start(f32[32,2,16,256]{3,2,1,0:T(8,128)} %shard_map.59), calls=%async_computation.1 | async-start | bytes 2097152 | tf_op jit(solution)/shard_map/all_to_all | solution.py:209
  181.6 0.1 shard_map.62
  181.7 1.9 collective-permute-start.9
  183.6 1.6 collective-permute-start.11
  185.2 1.6 collective-permute-start.10
  186.8 11.3 %collective-permute-done.9.across_ref = f32[32,16,256]{2,1,0:T(8,128)S(1)} collective-permute-done((f32[32,16,256]{2,1,0:T(8,128)S(1)}, f32[32,16,256]{2,1,0:T(8,128)S(1)}, u32[]{:S(2)}, u32[]{:S(2)}) %collective-permute-start.9) | collective-permute-done | bytes 524320 | tf_op jit(solution)/shard_map/ppermute | solution.py:220
  198.1 9.7 %collective-permute-done.11.below_ref = f32[32,16,256]{2,1,0:T(8,128)S(1)} collective-permute-done((f32[32,16,256]{2,1,0:T(8,128)S(1)}, f32[32,16,256]{2,1,0:T(8,128)S(1)}, u32[]{:S(2)}, u32[]{:S(2)}) %collective-permute-start.11) | collective-permute-done | bytes 524320 | tf_op jit(solution)/shard_map/ppermute | solution.py:220
  207.8 0.0 collective-permute-done.10.above_ref
  207.8 1.2 all-to-all-done.1.b_ref
  209.0 1.4 shard_map.63
  (3 shorter events, 0.0 us)
Async XLA Ops:
  2.9 16.6 %collective-permute-start.6 = (f32[32,16,256]{2,1,0:T(8,128)}, f32[32,16,256]{2,1,0:T(8,128)S(1)}, u32[]{:S(2)}, u32[]{:S(2)}) collective-permute-start(f32[32,16,256]{2,1,0:T(8,128)} %get-tuple-element.27.own_ref), channel_id=1, source_target_pairs={{0,128},{2,130},{4,132},{6,134},{16,144},{18,146},{20,148},{22,150... | collective-permute-start | bytes 1572872 | tf_op jit(solution)/shard_map/ppermute | solution.py:220
  6.2 23.4 %collective-permute-start.8 = (f32[32,16,256]{2,1,0:T(8,128)}, f32[32,16,256]{2,1,0:T(8,128)S(1)}, u32[]{:S(2)}, u32[]{:S(2)}) collective-permute-start(f32[32,16,256]{2,1,0:T(8,128)} %get-tuple-element.28), channel_id=1, source_target_pairs={{0,8},{2,10},{4,12},{6,14},{16,24},{18,26},{20,28},{22,30},{32,40}... | collective-permute-start | bytes 1572872 | tf_op jit(solution)/shard_map/ppermute | solution.py:220
  6.8 23.1 %collective-permute-start.7 = (f32[32,16,256]{2,1,0:T(8,128)}, f32[32,16,256]{2,1,0:T(8,128)S(1)}, u32[]{:S(2)}, u32[]{:S(2)}) collective-permute-start(f32[32,16,256]{2,1,0:T(8,128)} %get-tuple-element.28), channel_id=1, source_target_pairs={{0,136},{2,138},{4,140},{6,142},{16,152},{18,154},{20,156},{22,158... | collective-permute-start | bytes 1572872 | tf_op jit(solution)/shard_map/ppermute | solution.py:220
  30.0 1.0 copy-start.3
  31.1 44.5 %copy-start.9 = (f32[1,1024]{1,0:T(1,128)S(1)}, f32[1,1024]{1,0:T(1,128)}, u32[]{:S(2)}) copy-start(f32[1,1024]{1,0:T(1,128)} %param.8) | copy-start | bytes 12292
  69.2 32.4 %all-to-all-start = ((f32[32,2,16,256]{3,2,1,0:T(8,128)}), f32[32,2,16,256]{3,2,1,0:T(8,128)S(1)}, u32[]{:S(2)}, u32[]{:S(2)}) async-start(f32[32,2,16,256]{3,2,1,0:T(8,128)} %get-tuple-element.22), calls=%async_computation | async-start | bytes 2097152 | tf_op jit(solution)/shard_map/all_to_all | solution.py:209
  76.6 2.2 %copy-start = (f32[1,1024,1024]{2,1,0:T(8,128)S(1)}, f32[1,1024,1024]{2,1,0:T(8,128)}, u32[]{:S(2)}) copy-start(f32[1,1024,1024]{2,1,0:T(8,128)} %a_ref.1) | copy-start | bytes 12582916
  78.8 2.2 %copy-start.1 = (f32[1,1024,1024]{2,1,0:T(8,128)S(1)}, f32[1,1024,1024]{2,1,0:T(8,128)}, u32[]{:S(2)}) copy-start(f32[1,1024,1024]{2,1,0:T(8,128)} %s_ref.1) | copy-start | bytes 12582916
  82.4 1.3 copy-start.4
  83.7 1.3 copy-start.5
  85.0 1.3 copy-start.6
  86.4 1.4 copy-start.7
  101.5 70.3 %all-to-all-start.3 = ((f32[32,2,16,256]{3,2,1,0:T(8,128)}), f32[32,2,16,256]{3,2,1,0:T(8,128)S(1)}, u32[]{:S(2)}, u32[]{:S(2)}) async-start(f32[32,2,16,256]{3,2,1,0:T(8,128)} %shard_map.61), calls=%async_computation.3 | async-start | bytes 2097152 | tf_op jit(solution)/shard_map/all_to_all | solution.py:209
  108.1 25.1 %copy-start.8 = (f32[32,16,256]{2,1,0:T(8,128)}, f32[32,16,256]{2,1,0:T(8,128)S(1)}, u32[]{:S(2)}) copy-start(f32[32,16,256]{2,1,0:T(8,128)S(1)} %get-tuple-element.23.refs_6_) | copy-start | bytes 1572868
  108.1 16.4 %collective-permute-start = (f32[32,16,256]{2,1,0:T(8,128)S(1)}, f32[32,16,256]{2,1,0:T(8,128)S(1)}, u32[]{:S(2)}, u32[]{:S(2)}) collective-permute-start(f32[32,16,256]{2,1,0:T(8,128)S(1)} %get-tuple-element.23.refs_6_), channel_id=1, source_target_pairs={{0,128},{2,130},{4,132},{6,134},{16,144},{18,146},{20,148},{22,150... | collective-permute-start | bytes 1572872 | tf_op jit(solution)/shard_map/ppermute | solution.py:220
  109.8 22.6 %collective-permute-start.2 = (f32[32,16,256]{2,1,0:T(8,128)S(1)}, f32[32,16,256]{2,1,0:T(8,128)S(1)}, u32[]{:S(2)}, u32[]{:S(2)}) collective-permute-start(f32[32,16,256]{2,1,0:T(8,128)S(1)} %get-tuple-element.24), channel_id=1, source_target_pairs={{0,8},{2,10},{4,12},{6,14},{16,24},{18,26},{20,28},{22,30},{32,40}... | collective-permute-start | bytes 1572872 | tf_op jit(solution)/shard_map/ppermute | solution.py:220
  112.2 20.9 %collective-permute-start.1 = (f32[32,16,256]{2,1,0:T(8,128)S(1)}, f32[32,16,256]{2,1,0:T(8,128)S(1)}, u32[]{:S(2)}, u32[]{:S(2)}) collective-permute-start(f32[32,16,256]{2,1,0:T(8,128)S(1)} %get-tuple-element.24), channel_id=1, source_target_pairs={{0,136},{2,138},{4,140},{6,142},{16,152},{18,154},{20,156},{22,158... | collective-permute-start | bytes 1572872 | tf_op jit(solution)/shard_map/ppermute | solution.py:220
  124.5 8.7 %copy-start.10 = (f32[32,16,256]{2,1,0:T(8,128)}, f32[32,16,256]{2,1,0:T(8,128)S(1)}, u32[]{:S(2)}) copy-start(f32[32,16,256]{2,1,0:T(8,128)S(1)} %collective-permute-done.refs_7_) | copy-start | bytes 1572868
  132.4 0.8 copy-start.11
  133.2 0.8 copy-start.12
  142.8 16.6 %collective-permute-start.3 = (f32[32,16,256]{2,1,0:T(8,128)}, f32[32,16,256]{2,1,0:T(8,128)S(1)}, u32[]{:S(2)}, u32[]{:S(2)}) collective-permute-start(f32[32,16,256]{2,1,0:T(8,128)} %get-tuple-element.25.own_ref), channel_id=1, source_target_pairs={{0,128},{2,130},{4,132},{6,134},{16,144},{18,146},{20,148},{22,150... | collective-permute-start | bytes 1572872 | tf_op jit(solution)/shard_map/ppermute | solution.py:220
  144.7 25.0 %collective-permute-start.5 = (f32[32,16,256]{2,1,0:T(8,128)}, f32[32,16,256]{2,1,0:T(8,128)S(1)}, u32[]{:S(2)}, u32[]{:S(2)}) collective-permute-start(f32[32,16,256]{2,1,0:T(8,128)} %get-tuple-element.26), channel_id=1, source_target_pairs={{0,8},{2,10},{4,12},{6,14},{16,24},{18,26},{20,28},{22,30},{32,40}... | collective-permute-start | bytes 1572872 | tf_op jit(solution)/shard_map/ppermute | solution.py:220
  146.3 23.4 %collective-permute-start.4 = (f32[32,16,256]{2,1,0:T(8,128)}, f32[32,16,256]{2,1,0:T(8,128)S(1)}, u32[]{:S(2)}, u32[]{:S(2)}) collective-permute-start(f32[32,16,256]{2,1,0:T(8,128)} %get-tuple-element.26), channel_id=1, source_target_pairs={{0,136},{2,138},{4,140},{6,142},{16,152},{18,154},{20,156},{22,158... | collective-permute-start | bytes 1572872 | tf_op jit(solution)/shard_map/ppermute | solution.py:220
  169.7 1.0 copy-start.2
  171.8 37.2 %all-to-all-start.1 = ((f32[32,2,16,256]{3,2,1,0:T(8,128)}), f32[32,2,16,256]{3,2,1,0:T(8,128)S(1)}, u32[]{:S(2)}, u32[]{:S(2)}) async-start(f32[32,2,16,256]{3,2,1,0:T(8,128)} %shard_map.59), calls=%async_computation.1 | async-start | bytes 2097152 | tf_op jit(solution)/shard_map/all_to_all | solution.py:209
  181.7 16.4 %collective-permute-start.9 = (f32[32,16,256]{2,1,0:T(8,128)S(1)}, f32[32,16,256]{2,1,0:T(8,128)S(1)}, u32[]{:S(2)}, u32[]{:S(2)}) collective-permute-start(f32[32,16,256]{2,1,0:T(8,128)S(1)} %get-tuple-element.29.own_ref), channel_id=1, source_target_pairs={{0,128},{2,130},{4,132},{6,134},{16,144},{18,146},{20,148},{22,150... | collective-permute-start | bytes 1572872 | tf_op jit(solution)/shard_map/ppermute | solution.py:220
  183.6 24.2 %collective-permute-start.11 = (f32[32,16,256]{2,1,0:T(8,128)S(1)}, f32[32,16,256]{2,1,0:T(8,128)S(1)}, u32[]{:S(2)}, u32[]{:S(2)}) collective-permute-start(f32[32,16,256]{2,1,0:T(8,128)S(1)} %get-tuple-element.30), channel_id=1, source_target_pairs={{0,8},{2,10},{4,12},{6,14},{16,24},{18,26},{20,28},{22,30},{32,40}... | collective-permute-start | bytes 1572872 | tf_op jit(solution)/shard_map/ppermute | solution.py:220
  185.2 22.6 %collective-permute-start.10 = (f32[32,16,256]{2,1,0:T(8,128)S(1)}, f32[32,16,256]{2,1,0:T(8,128)S(1)}, u32[]{:S(2)}, u32[]{:S(2)}) collective-permute-start(f32[32,16,256]{2,1,0:T(8,128)S(1)} %get-tuple-element.30), channel_id=1, source_target_pairs={{0,136},{2,138},{4,140},{6,142},{16,152},{18,154},{20,156},{22,158... | collective-permute-start | bytes 1572872 | tf_op jit(solution)/shard_map/ppermute | solution.py:220

commit v2 on v1

--- a/solution.py
+++ b/solution.py
@@ -18,17 +18,19 @@
 PART = jax.ShapeDtypeStruct((ZX, ROWS, COLS), F32)
 WHOLE = jax.ShapeDtypeStruct((ZX, YL, ROWS, COLS), F32)
 CHUNKS = 4
-STEP = POINTS // CHUNKS
-GRANT = 58
-
-
-def call(kernel, inputs, outs, scratch=(), flops=0, grant=8, in_any=0, out_any=False):
+PIECES = 2
+STEP = POINTS // PIECES
+GRANT = 52
+OPEN = 50
+
+
+def call(kernel, inputs, outs, scratch=(), flops=0, grant=8, in_any=0, out_any=0):
     size = sum(v.size * 4 for v in (*inputs, *outs))
     return pl.pallas_call(
         kernel,
         out_shape=tuple(outs),
         in_specs=[ANY] * in_any + [VMEM] * (len(inputs) - in_any),
-        out_specs=tuple([ANY if out_any else VMEM] * len(outs)),
+        out_specs=tuple([ANY] * out_any + [VMEM] * (len(outs) - out_any)),
         scratch_shapes=list(scratch),
         compiler_params=pltpu.CompilerParams(vmem_limit_bytes=grant * MIB),
         cost_estimate=pl.CostEstimate(flops=flops, bytes_accessed=size, transcendentals=0),
@@ -51,24 +53,31 @@
     return (at // X) * YL * X + low * X + at % X
 
 
-def open_kernel(x_hbm, b_ref, own_ref, other_ref, x_ref, sems):
-    low = y_low()
-    width = WIDE // CHUNKS
-    copies = []
+def open_kernel(x_hbm, b_hbm, own_ref, other_ref, x_ref, b_ref, in_sems, out_sems):
+    low = y_low()
+    width, part = WIDE // CHUNKS, ZX // CHUNKS
+    arrivals, departures = [], []
     for c in range(CHUNKS):
         cols = pl.ds(c * width, width)
-        copies.append(pltpu.make_async_copy(x_hbm.at[:, :, cols], x_ref.at[:, :, cols], sems.at[c]))
-        copies[-1].start()
-    for at in range(ZX):
-        if at % (ZX // CHUNKS) == 0:
-            copies[at // (ZX // CHUNKS)].wait()
-        for yl in range(YL):
-            col = block_of(yl, at) * 2 * COLS
-            b_ref[at, yl] = x_ref[0, :, col + COLS : col + 2 * COLS]
+        source = x_hbm.at[:, :, cols]
+        arrivals.append(pltpu.make_async_copy(source, x_ref.at[:, :, cols], in_sems.at[c]))
+        arrivals[-1].start()
+    for c in range(CHUNKS):
+        arrivals[c].wait()
+        for at in range(c * part, c * part + part):
+            for yl in range(YL):
+                col = block_of(yl, at) * 2 * COLS
+                b_ref[at, yl] = x_ref[0, :, col + COLS : col + 2 * COLS]
+        rows = pl.ds(c * part, part)
+        departures.append(pltpu.make_async_copy(b_ref.at[rows], b_hbm.at[rows], out_sems.at[c]))
+        departures[-1].start()
+    for at in range(ZX):
         base = (at // X) * YL * X + at % X
         for ref, half in ((own_ref, low), (other_ref, 1 - low)):
             col = pl.multiple_of((base + half * X) * 2 * COLS, COLS)
             ref[at] = x_ref[0, :, pl.ds(col, COLS)]
+    for copy in departures:
+        copy.wait()
 
 
 def pick_kernel(in_ref, own_ref, other_ref):
@@ -124,13 +133,13 @@
 
 def fetch(sources, held, sems):
     for m in (0, 2):
-        for c in range(CHUNKS):
+        for c in range(PIECES):
             for i in (m, m + 1):
                 chunk(sources, held, sems, i, c).start()
 
 
 def solve(sources, held, sems, neg_ref, wave, fh, fl, ch, cl, done):
-    @pl.loop(0, CHUNKS)
+    @pl.loop(0, PIECES)
     def _(c):
         chunk(sources, held, sems, 0, c).wait()
         chunk(sources, held, sems, 1, c).wait()
@@ -138,7 +147,7 @@
         coefficients = product(held[0][rows], held[1][rows], fh, fl)
         ch[rows], cl[rows] = split(coefficients / (neg_ref[rows] + wave))
 
-    @pl.loop(0, CHUNKS)
+    @pl.loop(0, PIECES)
     def _(c):
         chunk(sources, held, sems, 2, c).wait()
         chunk(sources, held, sems, 3, c).wait()
@@ -230,7 +239,7 @@
 def body(right_side, analysis, synthesis, negated_eigen, wave_square):
     work = [
         *[pltpu.VMEM((POINTS, POINTS), BF16)] * 4,
-        pltpu.SemaphoreType.DMA((4, CHUNKS)),
+        pltpu.SemaphoreType.DMA((4, PIECES)),
         *[pltpu.VMEM((POINTS, COLS), BF16)] * 4,
         pltpu.VMEM((POINTS, COLS), F32),
     ]
@@ -240,9 +249,13 @@
     levels = (*matrices, negated_eigen.reshape(POINTS, 1), wave_square.reshape(1, 2 * COLS))
     held = [pltpu.VMEM((ROWS, WIDE), F32), pltpu.SemaphoreType.DMA((Z,))]
 
-    stage = [pltpu.VMEM((1, ROWS, WIDE), F32), pltpu.SemaphoreType.DMA((CHUNKS,))]
-
-    b, *a = call(open_kernel, [right_side], [WHOLE, PART, PART], stage, 0, GRANT, 1)
+    stage = [
+        pltpu.VMEM((1, ROWS, WIDE), F32),
+        pltpu.VMEM(WHOLE.shape, F32),
+        *[pltpu.SemaphoreType.DMA((CHUNKS,))] * 2,
+    ]
+
+    b, *a = call(open_kernel, [right_side], [WHOLE, PART, PART], stage, 0, OPEN, 1, 1)
     b = zx_exchange(b)
     a = y_exchange(*a)
     (a,) = call(fold_kernel, a, [WHOLE])
@@ -258,7 +271,7 @@
     b = zx_exchange(b)
     a = y_exchange(*a)
     out = jax.ShapeDtypeStruct((1, ROWS, WIDE), F32)
-    return call(close_kernel, [b, *a], [out], held, out_any=True)[0]
+    return call(close_kernel, [b, *a], [out], held, out_any=1)[0]
 
 
 def solution(mesh):

time: 212 us -> 208 us (0.981)
  local copies, waits for them, and re-layouts: 13.8 us -> 10.9 us
  Pallas kernels: 24.1 us -> 21.3 us
    pallas_call x9, Pallas kernels: 24.1 us -> 21.3 us  [call(): pl.pallas_call(kernel, out_shape=tuple(outs), in_specs=[ANY] * in_any + [...]
    unnamed x26 -> x24, local copies, waits for them, and re-layouts: 12.7 us -> 10.7 us
  transfers between devices with their start and end apart: 15 -> 15, of which waited for: 12 -> 12; matrix products, arithmetic and copies ran while one was open for 0% -> 0% of each run, Pallas kernels for 9% -> 8%
where the time goes in v2:
time: 208 us; the launch traced here: 206 us
  waiting for transfers between devices  91 us (44%)
  starting transfers between devices  44.5 us (21%)
  blocking collectives  38 us (18%)
  Pallas kernels  21.3 us (10%)
  local copies, waits for them, and re-layouts  10.9 us (5%)
    ppermute x12, waiting for transfers between devices, y_move(): return lax.ppermute(block, ('mirror', 'slab'), pairs)  83 us
    all_to_all x1, blocking collectives, zx_exchange(): lax.all_to_all(blocks, 'slab', split_axis=0, concat_axis=0, axis_index_gr...  38 us
    all_to_all x3, starting transfers between devices, zx_exchange(): lax.all_to_all(blocks, 'slab', split_axis=0, concat_axis=0, axis_index_gr...  22.8 us
    ppermute x12, starting transfers between devices, y_move(): return lax.ppermute(block, ('mirror', 'slab'), pairs)  21.7 us
    pallas_call x9, Pallas kernels, call(): pl.pallas_call(kernel, out_shape=tuple(outs), in_specs=[ANY] * in_any + [...  21.3 us
    unnamed x24, local copies, waits for them, and re-layouts  10.7 us
    all_to_all x3, waiting for transfers between devices, zx_exchange(): lax.all_to_all(blocks, 'slab', split_axis=0, concat_axis=0, axis_index_gr...  7.94 us
  transfers between devices with their start and end apart: 15, of which 12 were waited for; matrix products, arithmetic and copies ran while one was open for 0% of the time, Pallas kernels for 8%

profile of v2, /device:TPU:36, one launch (start us, length us, event | category | flops | bytes accessed | tf_op | source)
XLA Modules:
  0.0 206.1 jit_solution(15110855468287718393)
XLA Ops:
  0.0 2.3 %shard_map.56 = (f32[32,2,16,256]{3,2,1,0:T(8,128)}, f32[32,16,256]{2,1,0:T(8,128)S(1)}, f32[32,16,256]{2,1,0:T(8,128)S(1)}) custom-call(f32[1,16,32768]{2,1,0:T(8,128)} %x_hbm.1), custom_call_target="tpu_custom_call" | custom-call | bytes 4194304 | tf_op jit(solution)/shard_map/pallas_call | solution.py:29
  2.3 3.3 %collective-permute-start.6 = (f32[32,16,256]{2,1,0:T(8,128)S(1)}, f32[32,16,256]{2,1,0:T(8,128)S(1)}, u32[]{:S(2)}, u32[]{:S(2)}) collective-permute-start(f32[32,16,256]{2,1,0:T(8,128)S(1)} %get-tuple-element.27.own_ref), channel_id=1, source_target_pairs={{0,128},{2,130},{4,132},{6,134},{16,144},{18,146},{20,148},{22,150... | collective-permute-start | bytes 1572872 | tf_op jit(solution)/shard_map/ppermute | solution.py:229
  5.6 0.7 collective-permute-start.8
  6.3 2.6 %collective-permute-start.7 = (f32[32,16,256]{2,1,0:T(8,128)S(1)}, f32[32,16,256]{2,1,0:T(8,128)S(1)}, u32[]{:S(2)}, u32[]{:S(2)}) collective-permute-start(f32[32,16,256]{2,1,0:T(8,128)S(1)} %get-tuple-element.28), channel_id=1, source_target_pairs={{0,136},{2,138},{4,140},{6,142},{16,152},{18,154},{20,156},{22,158... | collective-permute-start | bytes 1572872 | tf_op jit(solution)/shard_map/ppermute | solution.py:229
  8.8 9.9 %collective-permute-done.6.across_ref = f32[32,16,256]{2,1,0:T(8,128)S(1)} collective-permute-done((f32[32,16,256]{2,1,0:T(8,128)S(1)}, f32[32,16,256]{2,1,0:T(8,128)S(1)}, u32[]{:S(2)}, u32[]{:S(2)}) %collective-permute-start.6) | collective-permute-done | bytes 524320 | tf_op jit(solution)/shard_map/ppermute | solution.py:229
  18.7 10.1 %collective-permute-done.8.below_ref = f32[32,16,256]{2,1,0:T(8,128)S(1)} collective-permute-done((f32[32,16,256]{2,1,0:T(8,128)S(1)}, f32[32,16,256]{2,1,0:T(8,128)S(1)}, u32[]{:S(2)}, u32[]{:S(2)}) %collective-permute-start.8) | collective-permute-done | bytes 524320 | tf_op jit(solution)/shard_map/ppermute | solution.py:229
  28.8 0.4 collective-permute-done.7.above_ref
  29.2 0.1 shard_map.60
  29.3 0.0 copy-start.8
  29.3 38.0 %all_to_all.20.refs_6_ = f32[32,2,16,256]{3,2,1,0:T(8,128)} all-to-all(f32[32,2,16,256]{3,2,1,0:T(8,128)S(1)} %shard_map.60), channel_id=1, replica_groups={{0,2,4,6,16,18,20,22,32,34,36,38,48,50,52,54,64,66,68,70,80,82,84,86,96..., dimensions={0} | all-to-all | bytes 2097152 | tf_op jit(solution)/shard_map/all_to_all | solution.py:218
  67.4 6.4 %all-to-all-start = ((f32[32,2,16,256]{3,2,1,0:T(8,128)}), f32[32,2,16,256]{3,2,1,0:T(8,128)S(1)}, u32[]{:S(2)}, u32[]{:S(2)}) async-start(f32[32,2,16,256]{3,2,1,0:T(8,128)} %get-tuple-element.22), calls=%async_computation | async-start | bytes 2097152 | tf_op jit(solution)/shard_map/all_to_all | solution.py:218
  73.8 0.0 copy-done.8
  73.8 0.2 copy.6.refs_4_
  74.0 0.0 copy-start
  74.1 2.2 %copy-done = f32[1,1024,1024]{2,1,0:T(8,128)S(1)} copy-done((f32[1,1024,1024]{2,1,0:T(8,128)S(1)}, f32[1,1024,1024]{2,1,0:T(8,128)}, u32[]{:S(2)}) %copy-start) | copy-done | bytes 4194328
  76.2 0.0 copy-start.1
  76.2 2.2 %copy-done.1 = f32[1,1024,1024]{2,1,0:T(8,128)S(1)} copy-done((f32[1,1024,1024]{2,1,0:T(8,128)S(1)}, f32[1,1024,1024]{2,1,0:T(8,128)}, u32[]{:S(2)}) %copy-start.1) | copy-done | bytes 4194328
  78.4 0.0 copy-start.7
  78.4 1.3 shard_map.55
  79.8 0.0 copy-start.2
  79.8 1.3 copy-done.2
  81.1 0.0 copy-start.3
  81.1 1.3 copy-done.3
  82.5 0.0 copy-start.4
  82.5 1.3 copy-done.4
  83.8 0.0 copy-start.5
  83.8 1.4 copy-done.5
  85.2 0.0 copy-done.7
  85.2 7.8 %shard_map.61 = f32[32,2,16,256]{3,2,1,0:T(8,128)} custom-call(bf16[1024,1024]{1,0:T(8,128)(2,1)} %copy-done.2, bf16[1024,1024]{1,0:T(8,128)(2,1)} %copy-done.3, bf16[1024,1024]{1,0:T(8,128)(2,1)} %copy-done.4, bf16[1024,1024]{1,0:T(8,128)(2,1)} %copy-done.5, f32[1024,1]{1,0:T(8,128)S(1)} %copy.6.refs_4_, f32[1,512]{1,0:T(1,128)S(1)} %bitcast.2, ...), custom_call_target="tpu_custom_call" | custom-call | flops 3221225472 | bytes 18880512 | tf_op jit(solution)/shard_map/pallas_call | solution.py:29
  93.0 6.8 %all-to-all-done.in_ref = f32[32,2,16,256]{3,2,1,0:T(8,128)S(1)} async-done(((f32[32,2,16,256]{3,2,1,0:T(8,128)}), f32[32,2,16,256]{3,2,1,0:T(8,128)S(1)}, u32[]{:S(2)}, u32[]{:S(2)}) %all-to-all-start) | async-done | bytes 1048608 | tf_op jit(solution)/shard_map/all_to_all | solution.py:218
  99.7 6.4 %all-to-all-start.3 = ((f32[32,2,16,256]{3,2,1,0:T(8,128)}), f32[32,2,16,256]{3,2,1,0:T(8,128)S(1)}, u32[]{:S(2)}, u32[]{:S(2)}) async-start(f32[32,2,16,256]{3,2,1,0:T(8,128)} %shard_map.61), calls=%async_computation.3 | async-start | bytes 2097152 | tf_op jit(solution)/shard_map/all_to_all | solution.py:218
  106.2 0.1 shard_map.57
  106.3 0.0 copy-start.6
  106.3 1.7 collective-permute-start
  108.0 2.4 %collective-permute-start.2 = (f32[32,16,256]{2,1,0:T(8,128)S(1)}, f32[32,16,256]{2,1,0:T(8,128)S(1)}, u32[]{:S(2)}, u32[]{:S(2)}) collective-permute-start(f32[32,16,256]{2,1,0:T(8,128)S(1)} %get-tuple-element.24), channel_id=1, source_target_pairs={{0,8},{2,10},{4,12},{6,14},{16,24},{18,26},{20,28},{22,30},{32,40}... | collective-permute-start | bytes 1572872 | tf_op jit(solution)/shard_map/ppermute | solution.py:229
  110.4 0.8 collective-permute-start.1
  111.2 11.5 %collective-permute-done.refs_7_ = f32[32,16,256]{2,1,0:T(8,128)S(1)} collective-permute-done((f32[32,16,256]{2,1,0:T(8,128)S(1)}, f32[32,16,256]{2,1,0:T(8,128)S(1)}, u32[]{:S(2)}, u32[]{:S(2)}) %collective-permute-start) | collective-permute-done | bytes 524320 | tf_op jit(solution)/shard_map/ppermute | solution.py:229
  122.7 0.0 copy-start.9
  122.7 8.0 %collective-permute-done.2.refs_9_ = f32[32,16,256]{2,1,0:T(8,128)S(1)} collective-permute-done((f32[32,16,256]{2,1,0:T(8,128)S(1)}, f32[32,16,256]{2,1,0:T(8,128)S(1)}, u32[]{:S(2)}, u32[]{:S(2)}) %collective-permute-start.2) | collective-permute-done | bytes 524320 | tf_op jit(solution)/shard_map/ppermute | solution.py:229
  130.6 0.0 copy-start.10
  130.6 0.7 collective-permute-done.1.refs_8_
  131.3 0.0 copy-done.6
  131.3 0.0 copy-done.9
  131.3 0.1 copy-done.10
  131.4 0.8 copy-done.11
  132.3 7.1 %shard_map.58 = (f32[32,16,256]{2,1,0:T(8,128)S(1)}, f32[32,16,256]{2,1,0:T(8,128)S(1)}) custom-call(bf16[1024,1024]{1,0:T(8,128)(2,1)} %copy-done.2, bf16[1024,1024]{1,0:T(8,128)(2,1)} %copy-done.3, bf16[1024,1024]{1,0:T(8,128)(2,1)} %copy-done.4, bf16[1024,1024]{1,0:T(8,128)(2,1)} %copy-done.5, f32[1024,1]{1,0:T(8,128)S(1)} %copy.6.refs_4_, ...), custom_call_target="tpu_custom_call" | custom-call | flops 3221225472 | bytes 19929088 | tf_op jit(solution)/shard_map/pallas_call | solution.py:29
  139.4 1.9 collective-permute-start.3
  141.3 1.6 collective-permute-start.5
  142.9 1.6 collective-permute-start.4
  144.5 11.3 %collective-permute-done.3.across_ref = f32[32,16,256]{2,1,0:T(8,128)S(1)} collective-permute-done((f32[32,16,256]{2,1,0:T(8,128)S(1)}, f32[32,16,256]{2,1,0:T(8,128)S(1)}, u32[]{:S(2)}, u32[]{:S(2)}) %collective-permute-start.3) | collective-permute-done | bytes 524320 | tf_op jit(solution)/shard_map/ppermute | solution.py:229
  155.9 10.2 %collective-permute-done.5.below_ref = f32[32,16,256]{2,1,0:T(8,128)S(1)} collective-permute-done((f32[32,16,256]{2,1,0:T(8,128)S(1)}, f32[32,16,256]{2,1,0:T(8,128)S(1)}, u32[]{:S(2)}, u32[]{:S(2)}) %collective-permute-start.5) | collective-permute-done | bytes 524320 | tf_op jit(solution)/shard_map/ppermute | solution.py:229
  166.1 0.0 collective-permute-done.4.above_ref
  166.1 1.1 shard_map.59
  167.2 0.0 all-to-all-done.3.in_ref
  167.2 10.0 %all-to-all-start.1 = ((f32[32,2,16,256]{3,2,1,0:T(8,128)}), f32[32,2,16,256]{3,2,1,0:T(8,128)S(1)}, u32[]{:S(2)}, u32[]{:S(2)}) async-start(f32[32,2,16,256]{3,2,1,0:T(8,128)} %shard_map.59), calls=%async_computation.1 | async-start | bytes 2097152 | tf_op jit(solution)/shard_map/all_to_all | solution.py:218
  177.2 0.1 shard_map.62
  177.2 1.9 collective-permute-start.9
  179.1 1.6 collective-permute-start.11
  180.7 1.6 collective-permute-start.10
  182.3 11.3 %collective-permute-done.9.across_ref = f32[32,16,256]{2,1,0:T(8,128)S(1)} collective-permute-done((f32[32,16,256]{2,1,0:T(8,128)S(1)}, f32[32,16,256]{2,1,0:T(8,128)S(1)}, u32[]{:S(2)}, u32[]{:S(2)}) %collective-permute-start.9) | collective-permute-done | bytes 524320 | tf_op jit(solution)/shard_map/ppermute | solution.py:229
  193.7 9.7 %collective-permute-done.11.below_ref = f32[32,16,256]{2,1,0:T(8,128)S(1)} collective-permute-done((f32[32,16,256]{2,1,0:T(8,128)S(1)}, f32[32,16,256]{2,1,0:T(8,128)S(1)}, u32[]{:S(2)}, u32[]{:S(2)}) %collective-permute-start.11) | collective-permute-done | bytes 524320 | tf_op jit(solution)/shard_map/ppermute | solution.py:229
  203.4 0.0 collective-permute-done.10.above_ref
  203.4 1.2 all-to-all-done.1.b_ref
  204.5 1.4 shard_map.63
  (1 shorter events, 0.0 us)
Async XLA Ops:
  2.3 16.4 %collective-permute-start.6 = (f32[32,16,256]{2,1,0:T(8,128)S(1)}, f32[32,16,256]{2,1,0:T(8,128)S(1)}, u32[]{:S(2)}, u32[]{:S(2)}) collective-permute-start(f32[32,16,256]{2,1,0:T(8,128)S(1)} %get-tuple-element.27.own_ref), channel_id=1, source_target_pairs={{0,128},{2,130},{4,132},{6,134},{16,144},{18,146},{20,148},{22,150... | collective-permute-start | bytes 1572872 | tf_op jit(solution)/shard_map/ppermute | solution.py:229
  5.6 23.2 %collective-permute-start.8 = (f32[32,16,256]{2,1,0:T(8,128)S(1)}, f32[32,16,256]{2,1,0:T(8,128)S(1)}, u32[]{:S(2)}, u32[]{:S(2)}) collective-permute-start(f32[32,16,256]{2,1,0:T(8,128)S(1)} %get-tuple-element.28), channel_id=1, source_target_pairs={{0,8},{2,10},{4,12},{6,14},{16,24},{18,26},{20,28},{22,30},{32,40}... | collective-permute-start | bytes 1572872 | tf_op jit(solution)/shard_map/ppermute | solution.py:229
  6.3 22.9 %collective-permute-start.7 = (f32[32,16,256]{2,1,0:T(8,128)S(1)}, f32[32,16,256]{2,1,0:T(8,128)S(1)}, u32[]{:S(2)}, u32[]{:S(2)}) collective-permute-start(f32[32,16,256]{2,1,0:T(8,128)S(1)} %get-tuple-element.28), channel_id=1, source_target_pairs={{0,136},{2,138},{4,140},{6,142},{16,152},{18,154},{20,156},{22,158... | collective-permute-start | bytes 1572872 | tf_op jit(solution)/shard_map/ppermute | solution.py:229
  29.3 44.5 %copy-start.8 = (f32[1,1024]{1,0:T(1,128)S(1)}, f32[1,1024]{1,0:T(1,128)}, u32[]{:S(2)}) copy-start(f32[1,1024]{1,0:T(1,128)} %param.8) | copy-start | bytes 12292
  67.4 32.4 %all-to-all-start = ((f32[32,2,16,256]{3,2,1,0:T(8,128)}), f32[32,2,16,256]{3,2,1,0:T(8,128)S(1)}, u32[]{:S(2)}, u32[]{:S(2)}) async-start(f32[32,2,16,256]{3,2,1,0:T(8,128)} %get-tuple-element.22), calls=%async_computation | async-start | bytes 2097152 | tf_op jit(solution)/shard_map/all_to_all | solution.py:218
  74.0 2.2 %copy-start = (f32[1,1024,1024]{2,1,0:T(8,128)S(1)}, f32[1,1024,1024]{2,1,0:T(8,128)}, u32[]{:S(2)}) copy-start(f32[1,1024,1024]{2,1,0:T(8,128)} %a_ref.1) | copy-start | bytes 12582916
  76.2 2.2 %copy-start.1 = (f32[1,1024,1024]{2,1,0:T(8,128)S(1)}, f32[1,1024,1024]{2,1,0:T(8,128)}, u32[]{:S(2)}) copy-start(f32[1,1024,1024]{2,1,0:T(8,128)} %s_ref.1) | copy-start | bytes 12582916
  78.4 6.7 %copy-start.7 = (f32[512]{0:T(512)S(1)}, f32[512]{0:T(512)}, u32[]{:S(2)}) copy-start(f32[512]{0:T(512)} %param.9) | copy-start | bytes 6148
  79.8 1.3 copy-start.2
  81.1 1.4 copy-start.3
  82.5 1.3 copy-start.4
  83.8 1.4 copy-start.5
  99.7 67.4 %all-to-all-start.3 = ((f32[32,2,16,256]{3,2,1,0:T(8,128)}), f32[32,2,16,256]{3,2,1,0:T(8,128)S(1)}, u32[]{:S(2)}, u32[]{:S(2)}) async-start(f32[32,2,16,256]{3,2,1,0:T(8,128)} %shard_map.61), calls=%async_computation.3 | async-start | bytes 2097152 | tf_op jit(solution)/shard_map/all_to_all | solution.py:218
  106.3 25.1 %copy-start.6 = (f32[32,16,256]{2,1,0:T(8,128)}, f32[32,16,256]{2,1,0:T(8,128)S(1)}, u32[]{:S(2)}) copy-start(f32[32,16,256]{2,1,0:T(8,128)S(1)} %get-tuple-element.23.refs_6_) | copy-start | bytes 1572868
  106.3 16.4 %collective-permute-start = (f32[32,16,256]{2,1,0:T(8,128)S(1)}, f32[32,16,256]{2,1,0:T(8,128)S(1)}, u32[]{:S(2)}, u32[]{:S(2)}) collective-permute-start(f32[32,16,256]{2,1,0:T(8,128)S(1)} %get-tuple-element.23.refs_6_), channel_id=1, source_target_pairs={{0,128},{2,130},{4,132},{6,134},{16,144},{18,146},{20,148},{22,150... | collective-permute-start | bytes 1572872 | tf_op jit(solution)/shard_map/ppermute | solution.py:229
  108.0 22.6 %collective-permute-start.2 = (f32[32,16,256]{2,1,0:T(8,128)S(1)}, f32[32,16,256]{2,1,0:T(8,128)S(1)}, u32[]{:S(2)}, u32[]{:S(2)}) collective-permute-start(f32[32,16,256]{2,1,0:T(8,128)S(1)} %get-tuple-element.24), channel_id=1, source_target_pairs={{0,8},{2,10},{4,12},{6,14},{16,24},{18,26},{20,28},{22,30},{32,40}... | collective-permute-start | bytes 1572872 | tf_op jit(solution)/shard_map/ppermute | solution.py:229
  110.4 20.9 %collective-permute-start.1 = (f32[32,16,256]{2,1,0:T(8,128)S(1)}, f32[32,16,256]{2,1,0:T(8,128)S(1)}, u32[]{:S(2)}, u32[]{:S(2)}) collective-permute-start(f32[32,16,256]{2,1,0:T(8,128)S(1)} %get-tuple-element.24), channel_id=1, source_target_pairs={{0,136},{2,138},{4,140},{6,142},{16,152},{18,154},{20,156},{22,158... | collective-permute-start | bytes 1572872 | tf_op jit(solution)/shard_map/ppermute | solution.py:229
  122.7 8.7 %copy-start.9 = (f32[32,16,256]{2,1,0:T(8,128)}, f32[32,16,256]{2,1,0:T(8,128)S(1)}, u32[]{:S(2)}) copy-start(f32[32,16,256]{2,1,0:T(8,128)S(1)} %collective-permute-done.refs_7_) | copy-start | bytes 1572868
  130.6 0.8 copy-start.10
  131.4 0.8 copy-start.11
  139.4 16.4 %collective-permute-start.3 = (f32[32,16,256]{2,1,0:T(8,128)S(1)}, f32[32,16,256]{2,1,0:T(8,128)S(1)}, u32[]{:S(2)}, u32[]{:S(2)}) collective-permute-start(f32[32,16,256]{2,1,0:T(8,128)S(1)} %get-tuple-element.25.own_ref), channel_id=1, source_target_pairs={{0,128},{2,130},{4,132},{6,134},{16,144},{18,146},{20,148},{22,150... | collective-permute-start | bytes 1572872 | tf_op jit(solution)/shard_map/ppermute | solution.py:229
  141.3 24.8 %collective-permute-start.5 = (f32[32,16,256]{2,1,0:T(8,128)S(1)}, f32[32,16,256]{2,1,0:T(8,128)S(1)}, u32[]{:S(2)}, u32[]{:S(2)}) collective-permute-start(f32[32,16,256]{2,1,0:T(8,128)S(1)} %get-tuple-element.26), channel_id=1, source_target_pairs={{0,8},{2,10},{4,12},{6,14},{16,24},{18,26},{20,28},{22,30},{32,40}... | collective-permute-start | bytes 1572872 | tf_op jit(solution)/shard_map/ppermute | solution.py:229
  142.9 23.2 %collective-permute-start.4 = (f32[32,16,256]{2,1,0:T(8,128)S(1)}, f32[32,16,256]{2,1,0:T(8,128)S(1)}, u32[]{:S(2)}, u32[]{:S(2)}) collective-permute-start(f32[32,16,256]{2,1,0:T(8,128)S(1)} %get-tuple-element.26), channel_id=1, source_target_pairs={{0,136},{2,138},{4,140},{6,142},{16,152},{18,154},{20,156},{22,158... | collective-permute-start | bytes 1572872 | tf_op jit(solution)/shard_map/ppermute | solution.py:229
  167.2 37.3 %all-to-all-start.1 = ((f32[32,2,16,256]{3,2,1,0:T(8,128)}), f32[32,2,16,256]{3,2,1,0:T(8,128)S(1)}, u32[]{:S(2)}, u32[]{:S(2)}) async-start(f32[32,2,16,256]{3,2,1,0:T(8,128)} %shard_map.59), calls=%async_computation.1 | async-start | bytes 2097152 | tf_op jit(solution)/shard_map/all_to_all | solution.py:218
  177.2 16.4 %collective-permute-start.9 = (f32[32,16,256]{2,1,0:T(8,128)S(1)}, f32[32,16,256]{2,1,0:T(8,128)S(1)}, u32[]{:S(2)}, u32[]{:S(2)}) collective-permute-start(f32[32,16,256]{2,1,0:T(8,128)S(1)} %get-tuple-element.29.own_ref), channel_id=1, source_target_pairs={{0,128},{2,130},{4,132},{6,134},{16,144},{18,146},{20,148},{22,150... | collective-permute-start | bytes 1572872 | tf_op jit(solution)/shard_map/ppermute | solution.py:229
  179.1 24.2 %collective-permute-start.11 = (f32[32,16,256]{2,1,0:T(8,128)S(1)}, f32[32,16,256]{2,1,0:T(8,128)S(1)}, u32[]{:S(2)}, u32[]{:S(2)}) collective-permute-start(f32[32,16,256]{2,1,0:T(8,128)S(1)} %get-tuple-element.30), channel_id=1, source_target_pairs={{0,8},{2,10},{4,12},{6,14},{16,24},{18,26},{20,28},{22,30},{32,40}... | collective-permute-start | bytes 1572872 | tf_op jit(solution)/shard_map/ppermute | solution.py:229
  180.7 22.6 %collective-permute-start.10 = (f32[32,16,256]{2,1,0:T(8,128)S(1)}, f32[32,16,256]{2,1,0:T(8,128)S(1)}, u32[]{:S(2)}, u32[]{:S(2)}) collective-permute-start(f32[32,16,256]{2,1,0:T(8,128)S(1)} %get-tuple-element.30), channel_id=1, source_target_pairs={{0,136},{2,138},{4,140},{6,142},{16,152},{18,154},{20,156},{22,158... | collective-permute-start | bytes 1572872 | tf_op jit(solution)/shard_map/ppermute | solution.py:229

commit v3 on v2

--- a/solution.py
+++ b/solution.py
@@ -131,43 +131,74 @@
     return pltpu.make_async_copy(sources[i].at[rows], held[i].at[rows], sems.at[i, c])
 
 
+def begin(sources, held, sems, m, c):
+    chunk(sources, held, sems, m, c).start()
+    chunk(sources, held, sems, m + 1, c).start()
+
+
+def arrive(sources, held, sems, m, c):
+    chunk(sources, held, sems, m, c).wait()
+    chunk(sources, held, sems, m + 1, c).wait()
+
+
 def fetch(sources, held, sems):
-    for m in (0, 2):
-        for c in range(PIECES):
-            for i in (m, m + 1):
-                chunk(sources, held, sems, i, c).start()
-
-
-def solve(sources, held, sems, neg_ref, wave, fh, fl, ch, cl, done):
+    for c in range(PIECES):
+        begin(sources, held, sems, 0, c)
+
+
+def solve(sources, held, sems, neg_ref, wave, fh, fl, ch, cl, done, ready=None):
     @pl.loop(0, PIECES)
     def _(c):
-        chunk(sources, held, sems, 0, c).wait()
-        chunk(sources, held, sems, 1, c).wait()
+        arrive(sources, held, sems, 0, c)
+
+        begin(sources, held, sems, 2, c)
         rows = pl.ds(pl.multiple_of(c * STEP, STEP), STEP)
         coefficients = product(held[0][rows], held[1][rows], fh, fl)
         ch[rows], cl[rows] = split(coefficients / (neg_ref[rows] + wave))
 
     @pl.loop(0, PIECES)
     def _(c):
-        chunk(sources, held, sems, 2, c).wait()
-        chunk(sources, held, sems, 3, c).wait()
+        arrive(sources, held, sems, 2, c)
         rows = pl.ds(pl.multiple_of(c * STEP, STEP), STEP)
         done[rows] = -product(held[2][rows], held[3][rows], ch, cl)
+        if ready is not None:
+            ready(c)
 
 
 def solve_a_kernel(*refs):
-    sources, (neg_ref, wave_ref, in_ref, out_ref) = refs[:4], refs[4:8]
-    held, sems, work = refs[8:12], refs[12], refs[13:]
+    sources, in_hbm, neg_ref, wave_ref, out_hbm = refs[:4], *refs[4:8]
+    held, sems, work = refs[8:12], refs[12], refs[13:18]
+    in_ref, out_ref, in_sems, out_sems = refs[18:]
+    fh, fl, _, _, done = work
+    part = ZX // PIECES
+    arrivals = []
+    for p in range(PIECES):
+        ats = pl.ds(p * part, part)
+        arrivals.append(pltpu.make_async_copy(in_hbm.at[ats], in_ref.at[ats], in_sems.at[p]))
+        arrivals[-1].start()
     fetch(sources, held, sems)
-    fh, fl, _, _, done = work
-    for at in range(ZX):
+    for at in range(ZX):
+        if at % part == 0:
+            arrivals[at // part].wait()
         for yl in range(YL):
             rows = pl.ds(row_of(yl, at), ROWS)
             fh[rows], fl[rows] = split(in_ref[at, yl] * 0.5)
-    solve(sources, held, sems, neg_ref, wave_ref[:, :COLS], *work)
-    for at in range(ZX):
-        for yl in range(YL):
-            out_ref[at, yl] = done[pl.ds(row_of(yl, at), ROWS)]
+
+    def leave(p):
+        ats = pl.ds(pl.multiple_of(p * part, part), part)
+        return pltpu.make_async_copy(out_ref.at[ats], out_hbm.at[ats], out_sems.at[p])
+
+    def ready(p):
+        base = p * part
+        for i in range(part):
+            for yl in range(YL):
+                rows = pl.ds(pl.multiple_of(p * STEP + row_of(yl, i), ROWS), ROWS)
+                out_ref[base + i, yl] = done[rows]
+        leave(p).start()
+
+    solve(sources, held, sems, neg_ref, wave_ref[:, :COLS], *work, ready)
+    for p in range(PIECES):
+        leave(p).wait()
 
 
 def solve_b_kernel(*refs):
@@ -263,7 +294,9 @@
     a = zx_exchange(a)
     b = y_exchange(*b)
     b = call(solve_b_kernel, [*levels, *b], [PART, PART], work, flops, GRANT, 4)
-    (a,) = call(solve_a_kernel, [*levels, a], [WHOLE], work, flops, GRANT, 4)
+    inputs = [*matrices, a, *levels[4:]]
+    own = [*[pltpu.VMEM(WHOLE.shape, F32)] * 2, *[pltpu.SemaphoreType.DMA((PIECES,))] * 2]
+    (a,) = call(solve_a_kernel, inputs, [WHOLE], work + own, flops, GRANT, 5, 1)
     a = zx_exchange(a)
     b = y_exchange(*b)
     (b,) = call(fold_kernel, b, [WHOLE])

time: 208 us -> 209 us (level)
  no operation moved by 1% of the time
where the time goes in v3:
time: 209 us; the launch traced here: 207 us
  waiting for transfers between devices  91.6 us (44%)
  starting transfers between devices  44.5 us (21%)
  blocking collectives  38 us (18%)
  Pallas kernels  21.1 us (10%)
  local copies, waits for them, and re-layouts  10.9 us (5%)
    ppermute x12, waiting for transfers between devices, y_move(): return lax.ppermute(block, ('mirror', 'slab'), pairs)  83 us
    all_to_all x1, blocking collectives, zx_exchange(): lax.all_to_all(blocks, 'slab', split_axis=0, concat_axis=0, axis_index_gr...  38 us
    all_to_all x3, starting transfers between devices, zx_exchange(): lax.all_to_all(blocks, 'slab', split_axis=0, concat_axis=0, axis_index_gr...  22.8 us
    ppermute x12, starting transfers between devices, y_move(): return lax.ppermute(block, ('mirror', 'slab'), pairs)  21.7 us
    pallas_call x9, Pallas kernels, call(): pl.pallas_call(kernel, out_shape=tuple(outs), in_specs=[ANY] * in_any + [...  21.1 us
    unnamed x24, local copies, waits for them, and re-layouts  10.7 us
    all_to_all x3, waiting for transfers between devices, zx_exchange(): lax.all_to_all(blocks, 'slab', split_axis=0, concat_axis=0, axis_index_gr...  8.61 us
  transfers between devices with their start and end apart: 15, of which 12 were waited for; matrix products, arithmetic and copies ran while one was open for 0% of the time, Pallas kernels for 8%

profile of v3, /device:TPU:36, one launch (start us, length us, event | category | flops | bytes accessed | tf_op | source)
XLA Modules:
  0.0 206.5 jit_solution(9100016498413344816)
XLA Ops:
  0.0 2.3 %shard_map.56 = (f32[32,2,16,256]{3,2,1,0:T(8,128)}, f32[32,16,256]{2,1,0:T(8,128)S(1)}, f32[32,16,256]{2,1,0:T(8,128)S(1)}) custom-call(f32[1,16,32768]{2,1,0:T(8,128)} %x_hbm.1), custom_call_target="tpu_custom_call" | custom-call | bytes 4194304 | tf_op jit(solution)/shard_map/pallas_call | solution.py:29
  2.3 3.3 %collective-permute-start.6 = (f32[32,16,256]{2,1,0:T(8,128)S(1)}, f32[32,16,256]{2,1,0:T(8,128)S(1)}, u32[]{:S(2)}, u32[]{:S(2)}) collective-permute-start(f32[32,16,256]{2,1,0:T(8,128)S(1)} %get-tuple-element.27.own_ref), channel_id=1, source_target_pairs={{0,128},{2,130},{4,132},{6,134},{16,144},{18,146},{20,148},{22,150... | collective-permute-start | bytes 1572872 | tf_op jit(solution)/shard_map/ppermute | solution.py:260
  5.6 0.7 collective-permute-start.8
  6.3 2.6 %collective-permute-start.7 = (f32[32,16,256]{2,1,0:T(8,128)S(1)}, f32[32,16,256]{2,1,0:T(8,128)S(1)}, u32[]{:S(2)}, u32[]{:S(2)}) collective-permute-start(f32[32,16,256]{2,1,0:T(8,128)S(1)} %get-tuple-element.28), channel_id=1, source_target_pairs={{0,136},{2,138},{4,140},{6,142},{16,152},{18,154},{20,156},{22,158... | collective-permute-start | bytes 1572872 | tf_op jit(solution)/shard_map/ppermute | solution.py:260
  8.8 9.9 %collective-permute-done.6.across_ref = f32[32,16,256]{2,1,0:T(8,128)S(1)} collective-permute-done((f32[32,16,256]{2,1,0:T(8,128)S(1)}, f32[32,16,256]{2,1,0:T(8,128)S(1)}, u32[]{:S(2)}, u32[]{:S(2)}) %collective-permute-start.6) | collective-permute-done | bytes 524320 | tf_op jit(solution)/shard_map/ppermute | solution.py:260
  18.7 10.1 %collective-permute-done.8.below_ref = f32[32,16,256]{2,1,0:T(8,128)S(1)} collective-permute-done((f32[32,16,256]{2,1,0:T(8,128)S(1)}, f32[32,16,256]{2,1,0:T(8,128)S(1)}, u32[]{:S(2)}, u32[]{:S(2)}) %collective-permute-start.8) | collective-permute-done | bytes 524320 | tf_op jit(solution)/shard_map/ppermute | solution.py:260
  28.8 0.4 collective-permute-done.7.above_ref
  29.2 0.1 shard_map.60
  29.3 0.0 copy-start.8
  29.3 38.0 %all_to_all.20.refs_4_ = f32[32,2,16,256]{3,2,1,0:T(8,128)} all-to-all(f32[32,2,16,256]{3,2,1,0:T(8,128)S(1)} %shard_map.60), channel_id=1, replica_groups={{0,2,4,6,16,18,20,22,32,34,36,38,48,50,52,54,64,66,68,70,80,82,84,86,96..., dimensions={0} | all-to-all | bytes 2097152 | tf_op jit(solution)/shard_map/all_to_all | solution.py:249
  67.4 6.4 %all-to-all-start = ((f32[32,2,16,256]{3,2,1,0:T(8,128)}), f32[32,2,16,256]{3,2,1,0:T(8,128)S(1)}, u32[]{:S(2)}, u32[]{:S(2)}) async-start(f32[32,2,16,256]{3,2,1,0:T(8,128)} %get-tuple-element.22), calls=%async_computation | async-start | bytes 2097152 | tf_op jit(solution)/shard_map/all_to_all | solution.py:249
  73.8 0.0 copy-done.8
  73.8 0.2 copy.6.refs_4_.refs_5_
  74.0 0.0 copy-start
  74.1 2.2 %copy-done = f32[1,1024,1024]{2,1,0:T(8,128)S(1)} copy-done((f32[1,1024,1024]{2,1,0:T(8,128)S(1)}, f32[1,1024,1024]{2,1,0:T(8,128)}, u32[]{:S(2)}) %copy-start) | copy-done | bytes 4194328
  76.2 0.0 copy-start.1
  76.2 2.2 %copy-done.1 = f32[1,1024,1024]{2,1,0:T(8,128)S(1)} copy-done((f32[1,1024,1024]{2,1,0:T(8,128)S(1)}, f32[1,1024,1024]{2,1,0:T(8,128)}, u32[]{:S(2)}) %copy-start.1) | copy-done | bytes 4194328
  78.4 0.0 copy-start.7
  78.4 1.3 shard_map.55
  79.8 0.0 copy-start.2
  79.8 1.3 copy-done.2
  81.1 0.0 copy-start.3
  81.1 1.3 copy-done.3
  82.5 0.0 copy-start.4
  82.5 1.3 copy-done.4
  83.8 0.0 copy-start.5
  83.8 1.4 copy-done.5
  85.2 0.0 copy-done.7
  85.2 7.1 %shard_map.61 = f32[32,2,16,256]{3,2,1,0:T(8,128)} custom-call(bf16[1024,1024]{1,0:T(8,128)(2,1)} %copy-done.2, bf16[1024,1024]{1,0:T(8,128)(2,1)} %copy-done.3, bf16[1024,1024]{1,0:T(8,128)(2,1)} %copy-done.4, bf16[1024,1024]{1,0:T(8,128)(2,1)} %copy-done.5, f32[32,2,16,256]{3,2,1,0:T(8,128)} %all_to_all.20.refs_4_, f32[1024,1]{1,0:T(8,128)S(1)} %copy.6.refs_4_.refs_5_, ...), custom_call_target="tpu_custom_call" | custom-call | flops 3221225472 | bytes 18880512 | tf_op jit(solution)/shard_map/pallas_call | solution.py:29
  92.3 7.4 %all-to-all-done.in_ref = f32[32,2,16,256]{3,2,1,0:T(8,128)S(1)} async-done(((f32[32,2,16,256]{3,2,1,0:T(8,128)}), f32[32,2,16,256]{3,2,1,0:T(8,128)S(1)}, u32[]{:S(2)}, u32[]{:S(2)}) %all-to-all-start) | async-done | bytes 1048608 | tf_op jit(solution)/shard_map/all_to_all | solution.py:249
  99.7 6.4 %all-to-all-start.3 = ((f32[32,2,16,256]{3,2,1,0:T(8,128)}), f32[32,2,16,256]{3,2,1,0:T(8,128)S(1)}, u32[]{:S(2)}, u32[]{:S(2)}) async-start(f32[32,2,16,256]{3,2,1,0:T(8,128)} %shard_map.61), calls=%async_computation.3 | async-start | bytes 2097152 | tf_op jit(solution)/shard_map/all_to_all | solution.py:249
  106.2 0.1 shard_map.57
  106.3 0.0 copy-start.6
  106.3 1.7 collective-permute-start
  108.0 2.4 %collective-permute-start.2 = (f32[32,16,256]{2,1,0:T(8,128)S(1)}, f32[32,16,256]{2,1,0:T(8,128)S(1)}, u32[]{:S(2)}, u32[]{:S(2)}) collective-permute-start(f32[32,16,256]{2,1,0:T(8,128)S(1)} %get-tuple-element.24), channel_id=1, source_target_pairs={{0,8},{2,10},{4,12},{6,14},{16,24},{18,26},{20,28},{22,30},{32,40}... | collective-permute-start | bytes 1572872 | tf_op jit(solution)/shard_map/ppermute | solution.py:260
  110.4 0.8 collective-permute-start.1
  111.2 11.5 %collective-permute-done.refs_7_ = f32[32,16,256]{2,1,0:T(8,128)S(1)} collective-permute-done((f32[32,16,256]{2,1,0:T(8,128)S(1)}, f32[32,16,256]{2,1,0:T(8,128)S(1)}, u32[]{:S(2)}, u32[]{:S(2)}) %collective-permute-start) | collective-permute-done | bytes 524320 | tf_op jit(solution)/shard_map/ppermute | solution.py:260
  122.7 0.0 copy-start.9
  122.7 8.0 %collective-permute-done.2.refs_9_ = f32[32,16,256]{2,1,0:T(8,128)S(1)} collective-permute-done((f32[32,16,256]{2,1,0:T(8,128)S(1)}, f32[32,16,256]{2,1,0:T(8,128)S(1)}, u32[]{:S(2)}, u32[]{:S(2)}) %collective-permute-start.2) | collective-permute-done | bytes 524320 | tf_op jit(solution)/shard_map/ppermute | solution.py:260
  130.6 0.0 copy-start.10
  130.6 0.7 collective-permute-done.1.refs_8_
  131.3 0.0 copy-done.6
  131.3 0.0 copy-done.9
  131.3 0.1 copy-done.10
  131.4 0.8 copy-done.11
  132.3 7.6 %shard_map.58 = (f32[32,16,256]{2,1,0:T(8,128)S(1)}, f32[32,16,256]{2,1,0:T(8,128)S(1)}) custom-call(bf16[1024,1024]{1,0:T(8,128)(2,1)} %copy-done.2, bf16[1024,1024]{1,0:T(8,128)(2,1)} %copy-done.3, bf16[1024,1024]{1,0:T(8,128)(2,1)} %copy-done.4, bf16[1024,1024]{1,0:T(8,128)(2,1)} %copy-done.5, f32[1024,1]{1,0:T(8,128)S(1)} %copy.6.refs_4_.refs_5_, ...), custom_call_target="tpu_custom_call" | custom-call | flops 3221225472 | bytes 19929088 | tf_op jit(solution)/shard_map/pallas_call | solution.py:29
  139.9 1.9 collective-permute-start.3
  141.7 1.6 collective-permute-start.5
  143.4 1.6 collective-permute-start.4
  145.0 11.3 %collective-permute-done.3.across_ref = f32[32,16,256]{2,1,0:T(8,128)S(1)} collective-permute-done((f32[32,16,256]{2,1,0:T(8,128)S(1)}, f32[32,16,256]{2,1,0:T(8,128)S(1)}, u32[]{:S(2)}, u32[]{:S(2)}) %collective-permute-start.3) | collective-permute-done | bytes 524320 | tf_op jit(solution)/shard_map/ppermute | solution.py:260
  156.3 10.2 %collective-permute-done.5.below_ref = f32[32,16,256]{2,1,0:T(8,128)S(1)} collective-permute-done((f32[32,16,256]{2,1,0:T(8,128)S(1)}, f32[32,16,256]{2,1,0:T(8,128)S(1)}, u32[]{:S(2)}, u32[]{:S(2)}) %collective-permute-start.5) | collective-permute-done | bytes 524320 | tf_op jit(solution)/shard_map/ppermute | solution.py:260
  166.5 0.0 collective-permute-done.4.above_ref
  166.5 1.1 shard_map.59
  167.6 0.0 all-to-all-done.3.in_ref
  167.6 10.0 %all-to-all-start.1 = ((f32[32,2,16,256]{3,2,1,0:T(8,128)}), f32[32,2,16,256]{3,2,1,0:T(8,128)S(1)}, u32[]{:S(2)}, u32[]{:S(2)}) async-start(f32[32,2,16,256]{3,2,1,0:T(8,128)} %shard_map.59), calls=%async_computation.1 | async-start | bytes 2097152 | tf_op jit(solution)/shard_map/all_to_all | solution.py:249
  177.6 0.1 shard_map.62
  177.7 1.9 collective-permute-start.9
  179.6 1.6 collective-permute-start.11
  181.2 1.6 collective-permute-start.10
  182.8 11.3 %collective-permute-done.9.across_ref = f32[32,16,256]{2,1,0:T(8,128)S(1)} collective-permute-done((f32[32,16,256]{2,1,0:T(8,128)S(1)}, f32[32,16,256]{2,1,0:T(8,128)S(1)}, u32[]{:S(2)}, u32[]{:S(2)}) %collective-permute-start.9) | collective-permute-done | bytes 524320 | tf_op jit(solution)/shard_map/ppermute | solution.py:260
  194.1 9.7 %collective-permute-done.11.below_ref = f32[32,16,256]{2,1,0:T(8,128)S(1)} collective-permute-done((f32[32,16,256]{2,1,0:T(8,128)S(1)}, f32[32,16,256]{2,1,0:T(8,128)S(1)}, u32[]{:S(2)}, u32[]{:S(2)}) %collective-permute-start.11) | collective-permute-done | bytes 524320 | tf_op jit(solution)/shard_map/ppermute | solution.py:260
  203.8 0.0 collective-permute-done.10.above_ref
  203.8 1.2 all-to-all-done.1.b_ref
  205.0 1.4 shard_map.63
  (1 shorter events, 0.0 us)
Async XLA Ops:
  2.3 16.4 %collective-permute-start.6 = (f32[32,16,256]{2,1,0:T(8,128)S(1)}, f32[32,16,256]{2,1,0:T(8,128)S(1)}, u32[]{:S(2)}, u32[]{:S(2)}) collective-permute-start(f32[32,16,256]{2,1,0:T(8,128)S(1)} %get-tuple-element.27.own_ref), channel_id=1, source_target_pairs={{0,128},{2,130},{4,132},{6,134},{16,144},{18,146},{20,148},{22,150... | collective-permute-start | bytes 1572872 | tf_op jit(solution)/shard_map/ppermute | solution.py:260
  5.6 23.2 %collective-permute-start.8 = (f32[32,16,256]{2,1,0:T(8,128)S(1)}, f32[32,16,256]{2,1,0:T(8,128)S(1)}, u32[]{:S(2)}, u32[]{:S(2)}) collective-permute-start(f32[32,16,256]{2,1,0:T(8,128)S(1)} %get-tuple-element.28), channel_id=1, source_target_pairs={{0,8},{2,10},{4,12},{6,14},{16,24},{18,26},{20,28},{22,30},{32,40}... | collective-permute-start | bytes 1572872 | tf_op jit(solution)/shard_map/ppermute | solution.py:260
  6.3 22.9 %collective-permute-start.7 = (f32[32,16,256]{2,1,0:T(8,128)S(1)}, f32[32,16,256]{2,1,0:T(8,128)S(1)}, u32[]{:S(2)}, u32[]{:S(2)}) collective-permute-start(f32[32,16,256]{2,1,0:T(8,128)S(1)} %get-tuple-element.28), channel_id=1, source_target_pairs={{0,136},{2,138},{4,140},{6,142},{16,152},{18,154},{20,156},{22,158... | collective-permute-start | bytes 1572872 | tf_op jit(solution)/shard_map/ppermute | solution.py:260
  29.3 44.5 %copy-start.8 = (f32[1,1024]{1,0:T(1,128)S(1)}, f32[1,1024]{1,0:T(1,128)}, u32[]{:S(2)}) copy-start(f32[1,1024]{1,0:T(1,128)} %param.8) | copy-start | bytes 12292
  67.4 32.4 %all-to-all-start = ((f32[32,2,16,256]{3,2,1,0:T(8,128)}), f32[32,2,16,256]{3,2,1,0:T(8,128)S(1)}, u32[]{:S(2)}, u32[]{:S(2)}) async-start(f32[32,2,16,256]{3,2,1,0:T(8,128)} %get-tuple-element.22), calls=%async_computation | async-start | bytes 2097152 | tf_op jit(solution)/shard_map/all_to_all | solution.py:249
  74.0 2.2 %copy-start = (f32[1,1024,1024]{2,1,0:T(8,128)S(1)}, f32[1,1024,1024]{2,1,0:T(8,128)}, u32[]{:S(2)}) copy-start(f32[1,1024,1024]{2,1,0:T(8,128)} %a_ref.1) | copy-start | bytes 12582916
  76.2 2.2 %copy-start.1 = (f32[1,1024,1024]{2,1,0:T(8,128)S(1)}, f32[1,1024,1024]{2,1,0:T(8,128)}, u32[]{:S(2)}) copy-start(f32[1,1024,1024]{2,1,0:T(8,128)} %s_ref.1) | copy-start | bytes 12582916
  78.4 6.7 %copy-start.7 = (f32[512]{0:T(512)S(1)}, f32[512]{0:T(512)}, u32[]{:S(2)}) copy-start(f32[512]{0:T(512)} %param.9) | copy-start | bytes 6148
  79.8 1.3 copy-start.2
  81.1 1.4 copy-start.3
  82.5 1.3 copy-start.4
  83.8 1.4 copy-start.5
  99.7 67.9 %all-to-all-start.3 = ((f32[32,2,16,256]{3,2,1,0:T(8,128)}), f32[32,2,16,256]{3,2,1,0:T(8,128)S(1)}, u32[]{:S(2)}, u32[]{:S(2)}) async-start(f32[32,2,16,256]{3,2,1,0:T(8,128)} %shard_map.61), calls=%async_computation.3 | async-start | bytes 2097152 | tf_op jit(solution)/shard_map/all_to_all | solution.py:249
  106.3 25.1 %copy-start.6 = (f32[32,16,256]{2,1,0:T(8,128)}, f32[32,16,256]{2,1,0:T(8,128)S(1)}, u32[]{:S(2)}) copy-start(f32[32,16,256]{2,1,0:T(8,128)S(1)} %get-tuple-element.23.refs_6_) | copy-start | bytes 1572868
  106.3 16.4 %collective-permute-start = (f32[32,16,256]{2,1,0:T(8,128)S(1)}, f32[32,16,256]{2,1,0:T(8,128)S(1)}, u32[]{:S(2)}, u32[]{:S(2)}) collective-permute-start(f32[32,16,256]{2,1,0:T(8,128)S(1)} %get-tuple-element.23.refs_6_), channel_id=1, source_target_pairs={{0,128},{2,130},{4,132},{6,134},{16,144},{18,146},{20,148},{22,150... | collective-permute-start | bytes 1572872 | tf_op jit(solution)/shard_map/ppermute | solution.py:260
  108.0 22.6 %collective-permute-start.2 = (f32[32,16,256]{2,1,0:T(8,128)S(1)}, f32[32,16,256]{2,1,0:T(8,128)S(1)}, u32[]{:S(2)}, u32[]{:S(2)}) collective-permute-start(f32[32,16,256]{2,1,0:T(8,128)S(1)} %get-tuple-element.24), channel_id=1, source_target_pairs={{0,8},{2,10},{4,12},{6,14},{16,24},{18,26},{20,28},{22,30},{32,40}... | collective-permute-start | bytes 1572872 | tf_op jit(solution)/shard_map/ppermute | solution.py:260
  110.4 20.9 %collective-permute-start.1 = (f32[32,16,256]{2,1,0:T(8,128)S(1)}, f32[32,16,256]{2,1,0:T(8,128)S(1)}, u32[]{:S(2)}, u32[]{:S(2)}) collective-permute-start(f32[32,16,256]{2,1,0:T(8,128)S(1)} %get-tuple-element.24), channel_id=1, source_target_pairs={{0,136},{2,138},{4,140},{6,142},{16,152},{18,154},{20,156},{22,158... | collective-permute-start | bytes 1572872 | tf_op jit(solution)/shard_map/ppermute | solution.py:260
  122.7 8.7 %copy-start.9 = (f32[32,16,256]{2,1,0:T(8,128)}, f32[32,16,256]{2,1,0:T(8,128)S(1)}, u32[]{:S(2)}) copy-start(f32[32,16,256]{2,1,0:T(8,128)S(1)} %collective-permute-done.refs_7_) | copy-start | bytes 1572868
  130.6 0.8 copy-start.10
  131.4 0.8 copy-start.11
  139.9 16.4 %collective-permute-start.3 = (f32[32,16,256]{2,1,0:T(8,128)S(1)}, f32[32,16,256]{2,1,0:T(8,128)S(1)}, u32[]{:S(2)}, u32[]{:S(2)}) collective-permute-start(f32[32,16,256]{2,1,0:T(8,128)S(1)} %get-tuple-element.25.own_ref), channel_id=1, source_target_pairs={{0,128},{2,130},{4,132},{6,134},{16,144},{18,146},{20,148},{22,150... | collective-permute-start | bytes 1572872 | tf_op jit(solution)/shard_map/ppermute | solution.py:260
  141.7 24.8 %collective-permute-start.5 = (f32[32,16,256]{2,1,0:T(8,128)S(1)}, f32[32,16,256]{2,1,0:T(8,128)S(1)}, u32[]{:S(2)}, u32[]{:S(2)}) collective-permute-start(f32[32,16,256]{2,1,0:T(8,128)S(1)} %get-tuple-element.26), channel_id=1, source_target_pairs={{0,8},{2,10},{4,12},{6,14},{16,24},{18,26},{20,28},{22,30},{32,40}... | collective-permute-start | bytes 1572872 | tf_op jit(solution)/shard_map/ppermute | solution.py:260
  143.4 23.2 %collective-permute-start.4 = (f32[32,16,256]{2,1,0:T(8,128)S(1)}, f32[32,16,256]{2,1,0:T(8,128)S(1)}, u32[]{:S(2)}, u32[]{:S(2)}) collective-permute-start(f32[32,16,256]{2,1,0:T(8,128)S(1)} %get-tuple-element.26), channel_id=1, source_target_pairs={{0,136},{2,138},{4,140},{6,142},{16,152},{18,154},{20,156},{22,158... | collective-permute-start | bytes 1572872 | tf_op jit(solution)/shard_map/ppermute | solution.py:260
  167.6 37.3 %all-to-all-start.1 = ((f32[32,2,16,256]{3,2,1,0:T(8,128)}), f32[32,2,16,256]{3,2,1,0:T(8,128)S(1)}, u32[]{:S(2)}, u32[]{:S(2)}) async-start(f32[32,2,16,256]{3,2,1,0:T(8,128)} %shard_map.59), calls=%async_computation.1 | async-start | bytes 2097152 | tf_op jit(solution)/shard_map/all_to_all | solution.py:249
  177.7 16.4 %collective-permute-start.9 = (f32[32,16,256]{2,1,0:T(8,128)S(1)}, f32[32,16,256]{2,1,0:T(8,128)S(1)}, u32[]{:S(2)}, u32[]{:S(2)}) collective-permute-start(f32[32,16,256]{2,1,0:T(8,128)S(1)} %get-tuple-element.29.own_ref), channel_id=1, source_target_pairs={{0,128},{2,130},{4,132},{6,134},{16,144},{18,146},{20,148},{22,150... | collective-permute-start | bytes 1572872 | tf_op jit(solution)/shard_map/ppermute | solution.py:260
  179.6 24.2 %collective-permute-start.11 = (f32[32,16,256]{2,1,0:T(8,128)S(1)}, f32[32,16,256]{2,1,0:T(8,128)S(1)}, u32[]{:S(2)}, u32[]{:S(2)}) collective-permute-start(f32[32,16,256]{2,1,0:T(8,128)S(1)} %get-tuple-element.30), channel_id=1, source_target_pairs={{0,8},{2,10},{4,12},{6,14},{16,24},{18,26},{20,28},{22,30},{32,40}... | collective-permute-start | bytes 1572872 | tf_op jit(solution)/shard_map/ppermute | solution.py:260
  181.2 22.6 %collective-permute-start.10 = (f32[32,16,256]{2,1,0:T(8,128)S(1)}, f32[32,16,256]{2,1,0:T(8,128)S(1)}, u32[]{:S(2)}, u32[]{:S(2)}) collective-permute-start(f32[32,16,256]{2,1,0:T(8,128)S(1)} %get-tuple-element.30), channel_id=1, source_target_pairs={{0,136},{2,138},{4,140},{6,142},{16,152},{18,154},{20,156},{22,158... | collective-permute-start | bytes 1572872 | tf_op jit(solution)/shard_map/ppermute | solution.py:260
